TPU v7x, 256 devices: a whole 4x4x8 slice. The times are simulated.
256 devices in a mesh: gx: 8 (over z), gy: 32 (over y, x, core).
Axes of the slice: x: 4, y: 4, z: 8, core: 2. Of those that a mesh axis runs over, the one named last changes fastest.
Arguments:
- rhs: float32 [4096, 8192], P('gx', 'gy'), may hold values from -6 to 6, as said below
- pressure: float32 [4096, 8192], P('gx', 'gy'), may hold values from -6 to 6
- wet_mask: int32 [4096, 8192], P('gx', 'gy'), may hold values 0 or 1
- bathy_class: int32 [4096, 8192], P('gx', 'gy'), may hold values from 0 to 7
Outputs:
- new_pressure: float32 [4096, 8192], P('gx', 'gy')
- final_residual: float32 [4096, 8192], P('gx', 'gy')
Inputs may be any that keep to these rules, and one draw needn't show every extreme that they name: `rhs`: real-valued and rough from cell to cell.
All inputs are finite; a program needn't handle non-finite values. No bound on the sum of `wet_mask` on one device may be relied on, other than what follows from the above.
Results may differ from a plain program's by a relative error of at most 0.0003.
Values sent between devices are 32-bit elements; how exact they have to be, the bound alone decides.
A program may use at most 128 MiB of HBM per device.

v0:
```python
import jax
import jax.numpy as jnp
from jax import lax
from jax.sharding import PartitionSpec as P

LEVELS = 4
SWEEPS = 12


damping = 0.01
relaxation = 0.8


def padded(x, sides, width):
    edges = {}
    for axis, dim in sides:
        count, length = (lax.axis_size(axis), x.shape[dim])
        up = [(i, (i + 1) % count) for i in range(count - 1)]
        last = lax.slice_in_dim(x, length - width, length, axis=dim)
        initial = lax.slice_in_dim(x, 0, width, axis=dim)
        edges[dim] = (
            lax.ppermute(last, axis, up),
            lax.ppermute(initial, axis, [(b, a) for a, b in up]),
        )
    done = []
    for _, dim in sides:
        low, high = edges[dim]
        around = [(width, width) if d in done else (0, 0) for d in range(x.ndim)]
        x = jnp.concatenate([jnp.pad(low, around), x, jnp.pad(high, around)], axis=dim)
        done.append(dim)
    return x


def extended(x, sides, width):
    for axis, dim in sides:
        count, length = (lax.axis_size(axis), x.shape[dim])
        up = [(i, (i + 1) % count) for i in range(count - 1)]
        down = [(j, i) for i, j in up]
        last = lax.slice_in_dim(x, length - width, length, axis=dim)
        initial = lax.slice_in_dim(x, 0, width, axis=dim)
        before = lax.ppermute(last, axis, up)
        after = lax.ppermute(initial, axis, down)
        x = jnp.concatenate([before, x, after], axis=dim)
    return x


def mean_blocks(field):
    height, width = field.shape
    return field.reshape(height // 2, 2, width // 2, 2).sum(axis=(1, 3)) * 0.25


def face_couplings(weight_pad, level_scale):
    middle = weight_pad[1:-1, 1:-1]
    to_north = level_scale * jnp.minimum(middle, weight_pad[:-2, 1:-1])
    to_south = level_scale * jnp.minimum(middle, weight_pad[2:, 1:-1])
    to_west = level_scale * jnp.minimum(middle, weight_pad[1:-1, :-2])
    to_east = level_scale * jnp.minimum(middle, weight_pad[1:-1, 2:])
    diagonal = damping + to_north + to_south + to_west + to_east
    return (to_north, to_south, to_west, to_east, diagonal)


def apply_operator(field_pad, coeffs):
    to_north, to_south, to_west, to_east, diagonal = coeffs
    middle = field_pad[1:-1, 1:-1]
    beside = to_north * field_pad[:-2, 1:-1] + to_south * field_pad[2:, 1:-1]
    beside = beside + to_west * field_pad[1:-1, :-2] + to_east * field_pad[1:-1, 2:]
    return diagonal * middle - beside


def jacobi_step(field_pad, source, coeffs):
    middle = field_pad[1:-1, 1:-1]
    return middle + relaxation * (source - apply_operator(field_pad, coeffs)) / coeffs[4]


def prolong(field):
    return jnp.repeat(jnp.repeat(field, 2, axis=0), 2, axis=1)


def fine_halo(field):
    return padded(field, (("gx", 0), ("gy", 1)), 1)


def coef_halo(field):
    return padded(field, (("gx", 0), ("gy", 1)), 1)


def pad_both(field):
    return jnp.pad(field, 1)


def coarse_solve(source, coeffs, pad_fn):

    def sweep(sweep_index, current):
        return jacobi_step(pad_fn(current), source, coeffs)

    return lax.fori_loop(0, SWEEPS, sweep, jnp.zeros_like(source))


def local(rhs, pressure, wet_mask, bathy_class):
    wet_cells = wet_mask.astype(jnp.float32)
    weight = wet_cells * (1.0 + 0.5 * bathy_class.astype(jnp.float32))
    source = wet_cells * rhs
    first_guess = wet_cells * pressure
    level_coeffs = []
    for level in range(LEVELS):
        level_coeffs.append(face_couplings(coef_halo(weight), 0.5**level))
        weight = mean_blocks(weight)
    sources = [source]
    iterates = []
    iterate = jacobi_step(fine_halo(first_guess), source, level_coeffs[0])
    for level in range(LEVELS):
        if level > 0:
            iterate = relaxation * sources[level] / level_coeffs[level][4]
        iterates.append(iterate)
        residual_now = sources[level] - apply_operator(fine_halo(iterate), level_coeffs[level])
        sources.append(mean_blocks(residual_now))
    coarse_source = sources[LEVELS]
    level_scale = 0.5**LEVELS
    tile_rows, tile_cols = coarse_source.shape
    depth = SWEEPS + 1
    stacked = jnp.stack((coarse_source, weight))
    widened = extended(stacked, (("gx", 1), ("gy", 2)), depth)
    wide_source = widened[0, 1:-1, 1:-1]
    wide_coeffs = face_couplings(widened[1], level_scale)
    wide_field = coarse_solve(wide_source, wide_coeffs, pad_both)
    correction = wide_field[SWEEPS : SWEEPS + tile_rows, SWEEPS : SWEEPS + tile_cols]
    current = correction
    for level in range(LEVELS - 1, -1, -1):
        summed = iterates[level] + prolong(current)
        current = jacobi_step(fine_halo(summed), sources[level], level_coeffs[level])
    final_residual = source - apply_operator(fine_halo(current), level_coeffs[0])
    return (current, final_residual)


def solution(mesh):
    placed = (P("gx", "gy"), P("gx", "gy"), P("gx", "gy"), P("gx", "gy"))
    return jax.shard_map(
        local, mesh=mesh, in_specs=placed, out_specs=(P("gx", "gy"), P("gx", "gy")), check_vma=False
    )
```

profile of v0, /device:TPU:8, one launch (start us, length us, event | category | flops | bytes accessed | tf_op | source)
XLA Modules:
  0.0 399.5 jit_solution(13424908922478313657)
XLA Ops:
  5.4 3.8 collective-permute-start
  12.5 5.8 %collective-permute-start.3 = (f32[512,1]{0,1:T(1,128)S(1)}, f32[512,1]{0,1:T(1,128)S(1)}, u32[]{:S(2)}, u32[]{:S(2)}) collective-permute-start(f32[512,1]{0,1:T(1,128)S(1)} %get-tuple-element.183), channel_id=1, source_target_pairs={{1,0},{2,1},{3,2},{4,3},{5,4},{6,5},{7,6},{8,7},{9,8},{10,9},{11,1... | collective-permute-start | bytes 6152 | tf_op jit(solution)/shard_map/ppermute | solution.py:23
  19.0 5.2 %collective-permute-start.4 = (f32[1,256]{0,1:T(8,128)}, f32[1,256]{0,1:T(8,128)}, u32[]{:S(2)}, u32[]{:S(2)}) collective-permute-start(f32[1,256]{0,1:T(8,128)} %get-tuple-element.191), channel_id=1, source_target_pairs={{0,32},{32,64},{64,96},{96,128},{128,160},{160,192},{192,224},{1,3... | collective-permute-start | bytes 3080 | tf_op jit(solution)/shard_map/ppermute | solution.py:22
  24.4 34.8 %reshape.74 = f32[256,2,128,2]{3,2,1,0:T(8,128)} reshape(f32[512,256]{1,0:T(8,128)S(1)} %copy.39) | data formatting | bytes 1048576 | tf_op jit(solution)/shard_map/reshape | solution.py:49
  59.2 13.2 %reduce_sum.73 = f32[256,128]{1,0:T(8,128)S(1)} reduce(f32[256,2,128,2]{3,2,1,0:T(8,128)} %reshape.74, f32[]{:T(128)} %constant.23.clone.1), dimensions={1,3}, to_apply=%region_1.2 | reduce | flops 98304 | bytes 655364 | tf_op jit(solution)/shard_map/reduce_sum | solution.py:49
  73.2 9.8 %mul.366 = f32[128,2,64,2]{3,2,1,0:T(8,128)} reshape(f32[256,128]{1,0:T(8,128)S(1)} %broadcast_multiply_fusion) | data formatting | bytes 262144 | tf_op jit(solution)/shard_map/mul | solution.py:49
  83.0 4.5 %reduce_sum.75 = f32[128,64]{1,0:T(8,128)S(1)} reduce(f32[128,2,64,2]{3,2,1,0:T(8,128)} %mul.366, f32[]{:T(128)} %constant.23.clone.1), dimensions={1,3}, to_apply=%region_3.4 | reduce | flops 24576 | bytes 163844 | tf_op jit(solution)/shard_map/reduce_sum | solution.py:49
  95.5 5.8 %collective-permute-start.7 = (f32[512,1]{0,1:T(1,128)S(1)}, f32[512,1]{0,1:T(1,128)S(1)}, u32[]{:S(2)}, u32[]{:S(2)}) collective-permute-start(f32[512,1]{0,1:T(1,128)S(1)} %get-tuple-element.190), channel_id=1, source_target_pairs={{1,0},{2,1},{3,2},{4,3},{5,4},{6,5},{7,6},{8,7},{9,8},{10,9},{11,1... | collective-permute-start | bytes 6152 | tf_op jit(solution)/shard_map/ppermute | solution.py:23
  104.5 3.5 fusion.55
  108.2 4.6 %collective-permute-start.8 = (f32[1,256]{0,1:T(8,128)S(1)}, f32[1,256]{0,1:T(8,128)S(1)}, u32[]{:S(2)}, u32[]{:S(2)}) collective-permute-start(f32[1,256]{0,1:T(8,128)S(1)} %get-tuple-element.181), channel_id=1, source_target_pairs={{0,32},{32,64},{64,96},{96,128},{128,160},{160,192},{192,224},{1,3... | collective-permute-start | bytes 3080 | tf_op jit(solution)/shard_map/ppermute | solution.py:22
  115.9 5.8 %collective-permute-start.11 = (f32[512,1]{0,1:T(1,128)S(1)}, f32[512,1]{0,1:T(1,128)S(1)}, u32[]{:S(2)}, u32[]{:S(2)}) collective-permute-start(f32[512,1]{0,1:T(1,128)S(1)} %get-tuple-element.180), channel_id=1, source_target_pairs={{1,0},{2,1},{3,2},{4,3},{5,4},{6,5},{7,6},{8,7},{9,8},{10,9},{11,1... | collective-permute-start | bytes 6152 | tf_op jit(solution)/shard_map/ppermute | solution.py:23
  121.7 2.1 collective-permute-start.15
  123.9 4.8 %collective-permute-start.12 = (f32[1,128]{1,0:T(1,128)S(1)}, f32[1,128]{1,0:T(1,128)S(1)}, u32[]{:S(2)}, u32[]{:S(2)}) collective-permute-start(f32[1,128]{1,0:T(1,128)S(1)} %get-tuple-element.204), channel_id=1, source_target_pairs={{0,32},{32,64},{64,96},{96,128},{128,160},{160,192},{192,224},{1,3... | collective-permute-start | bytes 1544 | tf_op jit(solution)/shard_map/ppermute | solution.py:22
  134.1 34.8 %reshape.73 = f32[256,2,128,2]{3,2,1,0:T(8,128)} reshape(f32[512,256]{1,0:T(8,128)S(1)} %copy.38) | data formatting | bytes 1048576 | tf_op jit(solution)/shard_map/reshape | solution.py:49
  168.9 13.3 %reduce_sum.72 = f32[256,128]{1,0:T(8,128)S(1)} reduce(f32[256,2,128,2]{3,2,1,0:T(8,128)} %reshape.73, f32[]{:T(128)} %constant.23.clone.1), dimensions={1,3}, to_apply=%region_0.1 | reduce | flops 98304 | bytes 655364 | tf_op jit(solution)/shard_map/reduce_sum | solution.py:49
  184.5 5.8 %collective-permute-start.19 = (f32[256,1]{1,0:T(8,128)S(1)}, f32[256,1]{1,0:T(8,128)S(1)}, u32[]{:S(2)}, u32[]{:S(2)}) collective-permute-start(f32[256,1]{1,0:T(8,128)S(1)} %get-tuple-element.198), channel_id=1, source_target_pairs={{1,0},{2,1},{3,2},{4,3},{5,4},{6,5},{7,6},{8,7},{9,8},{10,9},{11,1... | collective-permute-start | bytes 3080 | tf_op jit(solution)/shard_map/ppermute | solution.py:23
  190.3 5.8 %collective-permute-start.16 = (f32[1,128]{1,0:T(1,128)S(1)}, f32[1,128]{1,0:T(1,128)S(1)}, u32[]{:S(2)}, u32[]{:S(2)}) collective-permute-start(f32[1,128]{1,0:T(1,128)S(1)} %get-tuple-element.199), channel_id=1, source_target_pairs={{0,32},{32,64},{64,96},{96,128},{128,160},{160,192},{192,224},{1,3... | collective-permute-start | bytes 1544 | tf_op jit(solution)/shard_map/ppermute | solution.py:22
  200.1 2.7 collective-permute-done.17
  202.8 5.1 %collective-permute-start.20 = (f32[1,64]{1,0:T(1,128)S(1)}, f32[1,64]{1,0:T(1,128)S(1)}, u32[]{:S(2)}, u32[]{:S(2)}) collective-permute-start(f32[1,64]{1,0:T(1,128)S(1)} %get-tuple-element.216), channel_id=1, source_target_pairs={{0,32},{32,64},{64,96},{96,128},{128,160},{160,192},{192,224},{1,3... | collective-permute-start | bytes 776 | tf_op jit(solution)/shard_map/ppermute | solution.py:22
  209.2 6.2 %collective-permute-start.28 = (f32[1,32]{0,1:T(8,128)}, f32[1,32]{0,1:T(8,128)}, u32[]{:S(2)}, u32[]{:S(2)}) collective-permute-start(f32[1,32]{0,1:T(8,128)} %get-tuple-element.232), channel_id=1, source_target_pairs={{0,32},{32,64},{64,96},{96,128},{128,160},{160,192},{192,224},{1,3... | collective-permute-start | bytes 392 | tf_op jit(solution)/shard_map/ppermute | solution.py:22
  215.6 9.8 %reshape.75 = f32[128,2,64,2]{3,2,1,0:T(8,128)} reshape(f32[256,128]{1,0:T(8,128)S(1)} %fusion.86) | data formatting | bytes 262144 | tf_op jit(solution)/shard_map/reshape | solution.py:49
  225.4 4.5 %reduce_sum.74 = f32[128,64]{1,0:T(8,128)S(1)} reduce(f32[128,2,64,2]{3,2,1,0:T(8,128)} %reshape.75, f32[]{:T(128)} %constant.23.clone.1), dimensions={1,3}, to_apply=%region_2.3 | reduce | flops 24576 | bytes 163844 | tf_op jit(solution)/shard_map/reduce_sum | solution.py:49
  232.3 4.5 %collective-permute-start.24 = (f32[1,64]{1,0:T(1,128)S(1)}, f32[1,64]{1,0:T(1,128)S(1)}, u32[]{:S(2)}, u32[]{:S(2)}) collective-permute-start(f32[1,64]{1,0:T(1,128)S(1)} %get-tuple-element.211), channel_id=1, source_target_pairs={{0,32},{32,64},{64,96},{96,128},{128,160},{160,192},{192,224},{1,3... | collective-permute-start | bytes 776 | tf_op jit(solution)/shard_map/ppermute | solution.py:22
  238.1 5.5 %collective-permute-start.27 = (f32[128,1]{1,0:T(8,128)S(1)}, f32[128,1]{1,0:T(8,128)S(1)}, u32[]{:S(2)}, u32[]{:S(2)}) collective-permute-start(f32[128,1]{1,0:T(8,128)S(1)} %get-tuple-element.210), channel_id=1, source_target_pairs={{1,0},{2,1},{3,2},{4,3},{5,4},{6,5},{7,6},{8,7},{9,8},{10,9},{11,1... | collective-permute-start | bytes 1544 | tf_op jit(solution)/shard_map/ppermute | solution.py:23
  248.2 5.8 %collective-permute-start.31 = (f32[64,1]{0,1:T(1,128)}, f32[64,1]{0,1:T(1,128)}, u32[]{:S(2)}, u32[]{:S(2)}) collective-permute-start(f32[64,1]{0,1:T(1,128)} %get-tuple-element.229), channel_id=1, source_target_pairs={{1,0},{2,1},{3,2},{4,3},{5,4},{6,5},{7,6},{8,7},{9,8},{10,9},{11,1... | collective-permute-start | bytes 776 | tf_op jit(solution)/shard_map/ppermute | solution.py:23
  254.9 2.8 reshape.76
  259.8 5.2 %collective-permute-start.32 = (f32[1,32]{0,1:T(8,128)S(1)}, f32[1,32]{0,1:T(8,128)S(1)}, u32[]{:S(2)}, u32[]{:S(2)}) collective-permute-start(f32[1,32]{0,1:T(8,128)S(1)} %get-tuple-element.227), channel_id=1, source_target_pairs={{0,32},{32,64},{64,96},{96,128},{128,160},{160,192},{192,224},{1,3... | collective-permute-start | bytes 392 | tf_op jit(solution)/shard_map/ppermute | solution.py:22
  266.9 5.8 %collective-permute-start.35 = (f32[64,1]{0,1:T(1,128)S(1)}, f32[64,1]{0,1:T(1,128)S(1)}, u32[]{:S(2)}, u32[]{:S(2)}) collective-permute-start(f32[64,1]{0,1:T(1,128)S(1)} %get-tuple-element.226), channel_id=1, source_target_pairs={{1,0},{2,1},{3,2},{4,3},{5,4},{6,5},{7,6},{8,7},{9,8},{10,9},{11,1... | collective-permute-start | bytes 776 | tf_op jit(solution)/shard_map/ppermute | solution.py:23
  275.2 3.3 collective-permute-done.33
  280.2 3.9 collective-permute-start.36
  285.5 5.1 %collective-permute-done.37 = f32[2,13,16]{1,2,0:T(8,128)S(1)} collective-permute-done((f32[2,13,16]{1,2,0:T(8,128)S(1)}, f32[2,13,16]{1,2,0:T(8,128)S(1)}, u32[]{:S(2)}, u32[]{:S(2)}) %collective-permute-start.37) | collective-permute-done | bytes 1696 | tf_op jit(solution)/shard_map/ppermute | solution.py:42
  292.7 5.8 %collective-permute-start.39 = (f32[2,58,13]{1,2,0:T(8,128)S(1)}, f32[2,58,13]{1,2,0:T(8,128)S(1)}, u32[]{:S(2)}, u32[]{:S(2)}) collective-permute-start(f32[2,58,13]{1,2,0:T(8,128)S(1)} %get-tuple-element.222), channel_id=1, source_target_pairs={{1,0},{2,1},{3,2},{4,3},{5,4},{6,5},{7,6},{8,7},{9,8},{10,9},{11,1... | collective-permute-start | bytes 18104 | tf_op jit(solution)/shard_map/ppermute | solution.py:42
  302.4 5.1 %collective-permute-start.40 = (f32[1,32]{0,1:T(8,128)S(1)}, f32[1,32]{0,1:T(8,128)S(1)}, u32[]{:S(2)}, u32[]{:S(2)}) collective-permute-start(f32[1,32]{0,1:T(8,128)S(1)} %get-tuple-element.219), channel_id=1, source_target_pairs={{0,32},{32,64},{64,96},{96,128},{128,160},{160,192},{192,224},{1,3... | collective-permute-start | bytes 392 | tf_op jit(solution)/shard_map/ppermute | solution.py:22
  309.5 5.8 %collective-permute-start.43 = (f32[64,1]{0,1:T(1,128)S(1)}, f32[64,1]{0,1:T(1,128)S(1)}, u32[]{:S(2)}, u32[]{:S(2)}) collective-permute-start(f32[64,1]{0,1:T(1,128)S(1)} %get-tuple-element.218), channel_id=1, source_target_pairs={{1,0},{2,1},{3,2},{4,3},{5,4},{6,5},{7,6},{8,7},{9,8},{10,9},{11,1... | collective-permute-start | bytes 776 | tf_op jit(solution)/shard_map/ppermute | solution.py:23
  316.6 4.3 %collective-permute-done.41 = f32[1,32]{0,1:T(8,128)S(1)} collective-permute-done((f32[1,32]{0,1:T(8,128)S(1)}, f32[1,32]{0,1:T(8,128)S(1)}, u32[]{:S(2)}, u32[]{:S(2)}) %collective-permute-start.41) | collective-permute-done | bytes 160 | tf_op jit(solution)/shard_map/ppermute | solution.py:23
  324.1 5.8 %collective-permute-start.47 = (f32[128,1]{1,0:T(8,128)S(1)}, f32[128,1]{1,0:T(8,128)S(1)}, u32[]{:S(2)}, u32[]{:S(2)}) collective-permute-start(f32[128,1]{1,0:T(8,128)S(1)} %get-tuple-element.206), channel_id=1, source_target_pairs={{1,0},{2,1},{3,2},{4,3},{5,4},{6,5},{7,6},{8,7},{9,8},{10,9},{11,1... | collective-permute-start | bytes 1544 | tf_op jit(solution)/shard_map/ppermute | solution.py:23
  329.9 3.9 collective-permute-start.44
  335.1 4.2 %collective-permute-done.45 = f32[1,64]{1,0:T(1,128)S(1)} collective-permute-done((f32[1,64]{1,0:T(1,128)S(1)}, f32[1,64]{1,0:T(1,128)S(1)}, u32[]{:S(2)}, u32[]{:S(2)}) %collective-permute-start.45) | collective-permute-done | bytes 288 | tf_op jit(solution)/shard_map/ppermute | solution.py:23
  340.9 2.1 collective-permute-start.50
  343.1 5.8 %collective-permute-start.51 = (f32[256,1]{1,0:T(8,128)S(1)}, f32[256,1]{1,0:T(8,128)S(1)}, u32[]{:S(2)}, u32[]{:S(2)}) collective-permute-start(f32[256,1]{1,0:T(8,128)S(1)} %get-tuple-element.194), channel_id=1, source_target_pairs={{1,0},{2,1},{3,2},{4,3},{5,4},{6,5},{7,6},{8,7},{9,8},{10,9},{11,1... | collective-permute-start | bytes 3080 | tf_op jit(solution)/shard_map/ppermute | solution.py:23
  348.8 3.1 collective-permute-start.48
  353.3 4.2 %collective-permute-done.49 = f32[1,128]{1,0:T(1,128)S(1)} collective-permute-done((f32[1,128]{1,0:T(1,128)S(1)}, f32[1,128]{1,0:T(1,128)S(1)}, u32[]{:S(2)}, u32[]{:S(2)}) %collective-permute-start.49) | collective-permute-done | bytes 544 | tf_op jit(solution)/shard_map/ppermute | solution.py:23
  361.3 5.8 %collective-permute-start.55 = (f32[512,1]{0,1:T(1,128)S(1)}, f32[512,1]{0,1:T(1,128)S(1)}, u32[]{:S(2)}, u32[]{:S(2)}) collective-permute-start(f32[512,1]{0,1:T(1,128)S(1)} %get-tuple-element.176), channel_id=1, source_target_pairs={{1,0},{2,1},{3,2},{4,3},{5,4},{6,5},{7,6},{8,7},{9,8},{10,9},{11,1... | collective-permute-start | bytes 6152 | tf_op jit(solution)/shard_map/ppermute | solution.py:23
  367.2 3.1 collective-permute-start.52
  372.8 4.4 %collective-permute-done.53 = f32[1,256]{0,1:T(8,128)S(1)} collective-permute-done((f32[1,256]{0,1:T(8,128)S(1)}, f32[1,256]{0,1:T(8,128)S(1)}, u32[]{:S(2)}, u32[]{:S(2)}) %collective-permute-start.53) | collective-permute-done | bytes 1056 | tf_op jit(solution)/shard_map/ppermute | solution.py:23
  380.9 5.8 %collective-permute-start.59 = (f32[512,1]{0,1:T(1,128)S(1)}, f32[512,1]{0,1:T(1,128)S(1)}, u32[]{:S(2)}, u32[]{:S(2)}) collective-permute-start(f32[512,1]{0,1:T(1,128)S(1)} %get-tuple-element.172), channel_id=1, source_target_pairs={{1,0},{2,1},{3,2},{4,3},{5,4},{6,5},{7,6},{8,7},{9,8},{10,9},{11,1... | collective-permute-start | bytes 6152 | tf_op jit(solution)/shard_map/ppermute | solution.py:23
  386.8 3.1 collective-permute-start.56
  392.4 4.4 %collective-permute-done.57 = f32[1,256]{0,1:T(8,128)S(1)} collective-permute-done((f32[1,256]{0,1:T(8,128)S(1)}, f32[1,256]{0,1:T(8,128)S(1)}, u32[]{:S(2)}, u32[]{:S(2)}) %collective-permute-start.57) | collective-permute-done | bytes 1056 | tf_op jit(solution)/shard_map/ppermute | solution.py:23
  (251 shorter events, 88.7 us)
Async XLA Ops:
  5.4 86.8 %collective-permute-start = (f32[1,256]{0,1:T(8,128)}, f32[1,256]{0,1:T(8,128)S(1)}, u32[]{:S(2)}, u32[]{:S(2)}) collective-permute-start(f32[1,256]{0,1:T(8,128)} %get-tuple-element.186), channel_id=1, source_target_pairs={{0,32},{32,64},{64,96},{96,128},{128,160},{160,192},{192,224},{1,3... | collective-permute-start | bytes 3080 | tf_op jit(solution)/shard_map/ppermute | solution.py:22
  9.2 84.3 %collective-permute-start.1 = (f32[1,256]{0,1:T(8,128)}, f32[1,256]{0,1:T(8,128)}, u32[]{:S(2)}, u32[]{:S(2)}) collective-permute-start(f32[1,256]{0,1:T(8,128)} %get-tuple-element.185), channel_id=1, source_target_pairs={{32,0},{64,32},{96,64},{128,96},{160,128},{192,160},{224,192},{33,... | collective-permute-start | bytes 3080 | tf_op jit(solution)/shard_map/ppermute | solution.py:23
  10.5 93.9 %collective-permute-start.2 = (f32[512,1]{0,1:T(1,128)S(1)}, f32[512,1]{0,1:T(1,128)S(1)}, u32[]{:S(2)}, u32[]{:S(2)}) collective-permute-start(f32[512,1]{0,1:T(1,128)S(1)} %get-tuple-element.184), channel_id=1, source_target_pairs={{0,1},{1,2},{2,3},{3,4},{4,5},{5,6},{6,7},{7,8},{8,9},{9,10},{10,1... | collective-permute-start | bytes 6152 | tf_op jit(solution)/shard_map/ppermute | solution.py:22
  12.5 92.0 %collective-permute-start.3 = (f32[512,1]{0,1:T(1,128)S(1)}, f32[512,1]{0,1:T(1,128)S(1)}, u32[]{:S(2)}, u32[]{:S(2)}) collective-permute-start(f32[512,1]{0,1:T(1,128)S(1)} %get-tuple-element.183), channel_id=1, source_target_pairs={{1,0},{2,1},{3,2},{4,3},{5,4},{6,5},{7,6},{8,7},{9,8},{10,9},{11,1... | collective-permute-start | bytes 6152 | tf_op jit(solution)/shard_map/ppermute | solution.py:23
  19.0 76.5 %collective-permute-start.4 = (f32[1,256]{0,1:T(8,128)}, f32[1,256]{0,1:T(8,128)}, u32[]{:S(2)}, u32[]{:S(2)}) collective-permute-start(f32[1,256]{0,1:T(8,128)} %get-tuple-element.191), channel_id=1, source_target_pairs={{0,32},{32,64},{64,96},{96,128},{128,160},{160,192},{192,224},{1,3... | collective-permute-start | bytes 3080 | tf_op jit(solution)/shard_map/ppermute | solution.py:22
  92.2 10.3 %collective-permute-start.5 = (f32[1,256]{0,1:T(8,128)}, f32[1,256]{0,1:T(8,128)S(1)}, u32[]{:S(2)}, u32[]{:S(2)}) collective-permute-start(f32[1,256]{0,1:T(8,128)} %get-tuple-element.192), channel_id=1, source_target_pairs={{32,0},{64,32},{96,64},{128,96},{160,128},{192,160},{224,192},{33,... | collective-permute-start | bytes 3080 | tf_op jit(solution)/shard_map/ppermute | solution.py:23
  93.5 10.9 %collective-permute-start.6 = (f32[512,1]{0,1:T(1,128)S(1)}, f32[512,1]{0,1:T(1,128)S(1)}, u32[]{:S(2)}, u32[]{:S(2)}) collective-permute-start(f32[512,1]{0,1:T(1,128)S(1)} %get-tuple-element.189), channel_id=1, source_target_pairs={{0,1},{1,2},{2,3},{3,4},{4,5},{5,6},{6,7},{7,8},{8,9},{9,10},{10,1... | collective-permute-start | bytes 6152 | tf_op jit(solution)/shard_map/ppermute | solution.py:22
  95.5 9.0 %collective-permute-start.7 = (f32[512,1]{0,1:T(1,128)S(1)}, f32[512,1]{0,1:T(1,128)S(1)}, u32[]{:S(2)}, u32[]{:S(2)}) collective-permute-start(f32[512,1]{0,1:T(1,128)S(1)} %get-tuple-element.190), channel_id=1, source_target_pairs={{1,0},{2,1},{3,2},{4,3},{5,4},{6,5},{7,6},{8,7},{9,8},{10,9},{11,1... | collective-permute-start | bytes 6152 | tf_op jit(solution)/shard_map/ppermute | solution.py:23
  102.5 79.8 %collective-permute-start.14 = (f32[256,1]{1,0:T(8,128)}, f32[256,1]{1,0:T(8,128)S(1)}, u32[]{:S(2)}, u32[]{:S(2)}) collective-permute-start(f32[256,1]{1,0:T(8,128)} %get-tuple-element.201), channel_id=1, source_target_pairs={{0,1},{1,2},{2,3},{3,4},{4,5},{5,6},{6,7},{7,8},{8,9},{9,10},{10,1... | collective-permute-start | bytes 3080 | tf_op jit(solution)/shard_map/ppermute | solution.py:22
  108.2 13.6 %collective-permute-start.8 = (f32[1,256]{0,1:T(8,128)S(1)}, f32[1,256]{0,1:T(8,128)S(1)}, u32[]{:S(2)}, u32[]{:S(2)}) collective-permute-start(f32[1,256]{0,1:T(8,128)S(1)} %get-tuple-element.181), channel_id=1, source_target_pairs={{0,32},{32,64},{64,96},{96,128},{128,160},{160,192},{192,224},{1,3... | collective-permute-start | bytes 3080 | tf_op jit(solution)/shard_map/ppermute | solution.py:22
  112.7 11.1 %collective-permute-start.9 = (f32[1,256]{0,1:T(8,128)S(1)}, f32[1,256]{0,1:T(8,128)S(1)}, u32[]{:S(2)}, u32[]{:S(2)}) collective-permute-start(f32[1,256]{0,1:T(8,128)S(1)} %get-tuple-element.182), channel_id=1, source_target_pairs={{32,0},{64,32},{96,64},{128,96},{160,128},{192,160},{224,192},{33,... | collective-permute-start | bytes 3080 | tf_op jit(solution)/shard_map/ppermute | solution.py:23
  114.0 14.7 %collective-permute-start.10 = (f32[512,1]{0,1:T(1,128)S(1)}, f32[512,1]{0,1:T(1,128)S(1)}, u32[]{:S(2)}, u32[]{:S(2)}) collective-permute-start(f32[512,1]{0,1:T(1,128)S(1)} %get-tuple-element.179), channel_id=1, source_target_pairs={{0,1},{1,2},{2,3},{3,4},{4,5},{5,6},{6,7},{7,8},{8,9},{9,10},{10,1... | collective-permute-start | bytes 6152 | tf_op jit(solution)/shard_map/ppermute | solution.py:22
  115.9 14.1 %collective-permute-start.11 = (f32[512,1]{0,1:T(1,128)S(1)}, f32[512,1]{0,1:T(1,128)S(1)}, u32[]{:S(2)}, u32[]{:S(2)}) collective-permute-start(f32[512,1]{0,1:T(1,128)S(1)} %get-tuple-element.180), channel_id=1, source_target_pairs={{1,0},{2,1},{3,2},{4,3},{5,4},{6,5},{7,6},{8,7},{9,8},{10,9},{11,1... | collective-permute-start | bytes 6152 | tf_op jit(solution)/shard_map/ppermute | solution.py:23
  121.7 60.6 %collective-permute-start.15 = (f32[256,1]{1,0:T(8,128)}, f32[256,1]{1,0:T(8,128)S(1)}, u32[]{:S(2)}, u32[]{:S(2)}) collective-permute-start(f32[256,1]{1,0:T(8,128)} %get-tuple-element.202), channel_id=1, source_target_pairs={{1,0},{2,1},{3,2},{4,3},{5,4},{6,5},{7,6},{8,7},{9,8},{10,9},{11,1... | collective-permute-start | bytes 3080 | tf_op jit(solution)/shard_map/ppermute | solution.py:23
  123.9 58.4 %collective-permute-start.12 = (f32[1,128]{1,0:T(1,128)S(1)}, f32[1,128]{1,0:T(1,128)S(1)}, u32[]{:S(2)}, u32[]{:S(2)}) collective-permute-start(f32[1,128]{1,0:T(1,128)S(1)} %get-tuple-element.204), channel_id=1, source_target_pairs={{0,32},{32,64},{64,96},{96,128},{128,160},{160,192},{192,224},{1,3... | collective-permute-start | bytes 1544 | tf_op jit(solution)/shard_map/ppermute | solution.py:22
  128.7 53.5 %collective-permute-start.13 = (f32[1,128]{1,0:T(1,128)S(1)}, f32[1,128]{1,0:T(1,128)S(1)}, u32[]{:S(2)}, u32[]{:S(2)}) collective-permute-start(f32[1,128]{1,0:T(1,128)S(1)} %get-tuple-element.203), channel_id=1, source_target_pairs={{32,0},{64,32},{96,64},{128,96},{160,128},{192,160},{224,192},{33,... | collective-permute-start | bytes 1544 | tf_op jit(solution)/shard_map/ppermute | solution.py:23
  130.0 100.0 %collective-permute-start.22 = (f32[128,1]{1,0:T(8,128)}, f32[128,1]{1,0:T(8,128)S(1)}, u32[]{:S(2)}, u32[]{:S(2)}) collective-permute-start(f32[128,1]{1,0:T(8,128)} %get-tuple-element.213), channel_id=1, source_target_pairs={{0,1},{1,2},{2,3},{3,4},{4,5},{5,6},{6,7},{7,8},{8,9},{9,10},{10,1... | collective-permute-start | bytes 1544 | tf_op jit(solution)/shard_map/ppermute | solution.py:22
  182.6 25.3 %collective-permute-start.18 = (f32[256,1]{1,0:T(8,128)S(1)}, f32[256,1]{1,0:T(8,128)S(1)}, u32[]{:S(2)}, u32[]{:S(2)}) collective-permute-start(f32[256,1]{1,0:T(8,128)S(1)} %get-tuple-element.197), channel_id=1, source_target_pairs={{0,1},{1,2},{2,3},{3,4},{4,5},{5,6},{6,7},{7,8},{8,9},{9,10},{10,1... | collective-permute-start | bytes 3080 | tf_op jit(solution)/shard_map/ppermute | solution.py:22
  184.5 24.6 %collective-permute-start.19 = (f32[256,1]{1,0:T(8,128)S(1)}, f32[256,1]{1,0:T(8,128)S(1)}, u32[]{:S(2)}, u32[]{:S(2)}) collective-permute-start(f32[256,1]{1,0:T(8,128)S(1)} %get-tuple-element.198), channel_id=1, source_target_pairs={{1,0},{2,1},{3,2},{4,3},{5,4},{6,5},{7,6},{8,7},{9,8},{10,9},{11,1... | collective-permute-start | bytes 3080 | tf_op jit(solution)/shard_map/ppermute | solution.py:23
  190.3 7.7 %collective-permute-start.16 = (f32[1,128]{1,0:T(1,128)S(1)}, f32[1,128]{1,0:T(1,128)S(1)}, u32[]{:S(2)}, u32[]{:S(2)}) collective-permute-start(f32[1,128]{1,0:T(1,128)S(1)} %get-tuple-element.199), channel_id=1, source_target_pairs={{0,32},{32,64},{64,96},{96,128},{128,160},{160,192},{192,224},{1,3... | collective-permute-start | bytes 1544 | tf_op jit(solution)/shard_map/ppermute | solution.py:22
  198.0 32.1 %collective-permute-start.23 = (f32[128,1]{1,0:T(8,128)S(1)}, f32[128,1]{1,0:T(8,128)S(1)}, u32[]{:S(2)}, u32[]{:S(2)}) collective-permute-start(f32[128,1]{1,0:T(8,128)S(1)} %copy-done.14), channel_id=1, source_target_pairs={{1,0},{2,1},{3,2},{4,3},{5,4},{6,5},{7,6},{8,7},{9,8},{10,9},{11,1... | collective-permute-start | bytes 1544 | tf_op jit(solution)/shard_map/ppermute | solution.py:23
  202.8 27.3 %collective-permute-start.20 = (f32[1,64]{1,0:T(1,128)S(1)}, f32[1,64]{1,0:T(1,128)S(1)}, u32[]{:S(2)}, u32[]{:S(2)}) collective-permute-start(f32[1,64]{1,0:T(1,128)S(1)} %get-tuple-element.216), channel_id=1, source_target_pairs={{0,32},{32,64},{64,96},{96,128},{128,160},{160,192},{192,224},{1,3... | collective-permute-start | bytes 776 | tf_op jit(solution)/shard_map/ppermute | solution.py:22
  207.9 22.2 %collective-permute-start.21 = (f32[1,64]{1,0:T(1,128)S(1)}, f32[1,64]{1,0:T(1,128)S(1)}, u32[]{:S(2)}, u32[]{:S(2)}) collective-permute-start(f32[1,64]{1,0:T(1,128)S(1)} %get-tuple-element.215), channel_id=1, source_target_pairs={{32,0},{64,32},{96,64},{128,96},{160,128},{192,160},{224,192},{33,... | collective-permute-start | bytes 776 | tf_op jit(solution)/shard_map/ppermute | solution.py:23
  209.2 49.5 %collective-permute-start.28 = (f32[1,32]{0,1:T(8,128)}, f32[1,32]{0,1:T(8,128)}, u32[]{:S(2)}, u32[]{:S(2)}) collective-permute-start(f32[1,32]{0,1:T(8,128)} %get-tuple-element.232), channel_id=1, source_target_pairs={{0,32},{32,64},{64,96},{96,128},{128,160},{160,192},{192,224},{1,3... | collective-permute-start | bytes 392 | tf_op jit(solution)/shard_map/ppermute | solution.py:22
  230.3 17.8 %collective-permute-start.26 = (f32[128,1]{1,0:T(8,128)S(1)}, f32[128,1]{1,0:T(8,128)S(1)}, u32[]{:S(2)}, u32[]{:S(2)}) collective-permute-start(f32[128,1]{1,0:T(8,128)S(1)} %get-tuple-element.209), channel_id=1, source_target_pairs={{0,1},{1,2},{2,3},{3,4},{4,5},{5,6},{6,7},{7,8},{8,9},{9,10},{10,1... | collective-permute-start | bytes 1544 | tf_op jit(solution)/shard_map/ppermute | solution.py:22
  232.3 12.7 %collective-permute-start.24 = (f32[1,64]{1,0:T(1,128)S(1)}, f32[1,64]{1,0:T(1,128)S(1)}, u32[]{:S(2)}, u32[]{:S(2)}) collective-permute-start(f32[1,64]{1,0:T(1,128)S(1)} %get-tuple-element.211), channel_id=1, source_target_pairs={{0,32},{32,64},{64,96},{96,128},{128,160},{160,192},{192,224},{1,3... | collective-permute-start | bytes 776 | tf_op jit(solution)/shard_map/ppermute | solution.py:22
  236.8 9.4 %collective-permute-start.25 = (f32[1,64]{1,0:T(1,128)S(1)}, f32[1,64]{1,0:T(1,128)S(1)}, u32[]{:S(2)}, u32[]{:S(2)}) collective-permute-start(f32[1,64]{1,0:T(1,128)S(1)} %get-tuple-element.212), channel_id=1, source_target_pairs={{32,0},{64,32},{96,64},{128,96},{160,128},{192,160},{224,192},{33,... | collective-permute-start | bytes 776 | tf_op jit(solution)/shard_map/ppermute | solution.py:23
  238.1 15.8 %collective-permute-start.27 = (f32[128,1]{1,0:T(8,128)S(1)}, f32[128,1]{1,0:T(8,128)S(1)}, u32[]{:S(2)}, u32[]{:S(2)}) collective-permute-start(f32[128,1]{1,0:T(8,128)S(1)} %get-tuple-element.210), channel_id=1, source_target_pairs={{1,0},{2,1},{3,2},{4,3},{5,4},{6,5},{7,6},{8,7},{9,8},{10,9},{11,1... | collective-permute-start | bytes 1544 | tf_op jit(solution)/shard_map/ppermute | solution.py:23
  244.9 13.8 %collective-permute-start.29 = (f32[1,32]{0,1:T(8,128)}, f32[1,32]{0,1:T(8,128)}, u32[]{:S(2)}, u32[]{:S(2)}) collective-permute-start(f32[1,32]{0,1:T(8,128)} %get-tuple-element.231), channel_id=1, source_target_pairs={{32,0},{64,32},{96,64},{128,96},{160,128},{192,160},{224,192},{33,... | collective-permute-start | bytes 392 | tf_op jit(solution)/shard_map/ppermute | solution.py:23
  246.2 12.5 %collective-permute-start.30 = (f32[64,1]{0,1:T(1,128)}, f32[64,1]{0,1:T(1,128)}, u32[]{:S(2)}, u32[]{:S(2)}) collective-permute-start(f32[64,1]{0,1:T(1,128)} %get-tuple-element.230), channel_id=1, source_target_pairs={{0,1},{1,2},{2,3},{3,4},{4,5},{5,6},{6,7},{7,8},{8,9},{9,10},{10,1... | collective-permute-start | bytes 776 | tf_op jit(solution)/shard_map/ppermute | solution.py:22
  248.2 10.5 %collective-permute-start.31 = (f32[64,1]{0,1:T(1,128)}, f32[64,1]{0,1:T(1,128)}, u32[]{:S(2)}, u32[]{:S(2)}) collective-permute-start(f32[64,1]{0,1:T(1,128)} %get-tuple-element.229), channel_id=1, source_target_pairs={{1,0},{2,1},{3,2},{4,3},{5,4},{6,5},{7,6},{8,7},{9,8},{10,9},{11,1... | collective-permute-start | bytes 776 | tf_op jit(solution)/shard_map/ppermute | solution.py:23
  259.8 15.4 %collective-permute-start.32 = (f32[1,32]{0,1:T(8,128)S(1)}, f32[1,32]{0,1:T(8,128)S(1)}, u32[]{:S(2)}, u32[]{:S(2)}) collective-permute-start(f32[1,32]{0,1:T(8,128)S(1)} %get-tuple-element.227), channel_id=1, source_target_pairs={{0,32},{32,64},{64,96},{96,128},{128,160},{160,192},{192,224},{1,3... | collective-permute-start | bytes 392 | tf_op jit(solution)/shard_map/ppermute | solution.py:22
  265.0 13.5 %collective-permute-start.34 = (f32[64,1]{0,1:T(1,128)S(1)}, f32[64,1]{0,1:T(1,128)S(1)}, u32[]{:S(2)}, u32[]{:S(2)}) collective-permute-start(f32[64,1]{0,1:T(1,128)S(1)} %get-tuple-element.225), channel_id=1, source_target_pairs={{0,1},{1,2},{2,3},{3,4},{4,5},{5,6},{6,7},{7,8},{8,9},{9,10},{10,1... | collective-permute-start | bytes 776 | tf_op jit(solution)/shard_map/ppermute | solution.py:22
  266.9 11.6 %collective-permute-start.35 = (f32[64,1]{0,1:T(1,128)S(1)}, f32[64,1]{0,1:T(1,128)S(1)}, u32[]{:S(2)}, u32[]{:S(2)}) collective-permute-start(f32[64,1]{0,1:T(1,128)S(1)} %get-tuple-element.226), channel_id=1, source_target_pairs={{1,0},{2,1},{3,2},{4,3},{5,4},{6,5},{7,6},{8,7},{9,8},{10,9},{11,1... | collective-permute-start | bytes 776 | tf_op jit(solution)/shard_map/ppermute | solution.py:23
  290.7 7.7 %collective-permute-start.38 = (f32[2,58,13]{1,2,0:T(8,128)S(1)}, f32[2,58,13]{1,2,0:T(8,128)S(1)}, u32[]{:S(2)}, u32[]{:S(2)}) collective-permute-start(f32[2,58,13]{1,2,0:T(8,128)S(1)} %get-tuple-element.221), channel_id=1, source_target_pairs={{0,1},{1,2},{2,3},{3,4},{4,5},{5,6},{6,7},{7,8},{8,9},{9,10},{10,1... | collective-permute-start | bytes 18104 | tf_op jit(solution)/shard_map/ppermute | solution.py:41
  292.7 7.2 %collective-permute-start.39 = (f32[2,58,13]{1,2,0:T(8,128)S(1)}, f32[2,58,13]{1,2,0:T(8,128)S(1)}, u32[]{:S(2)}, u32[]{:S(2)}) collective-permute-start(f32[2,58,13]{1,2,0:T(8,128)S(1)} %get-tuple-element.222), channel_id=1, source_target_pairs={{1,0},{2,1},{3,2},{4,3},{5,4},{6,5},{7,6},{8,7},{9,8},{10,9},{11,1... | collective-permute-start | bytes 18104 | tf_op jit(solution)/shard_map/ppermute | solution.py:42
  302.4 14.1 %collective-permute-start.40 = (f32[1,32]{0,1:T(8,128)S(1)}, f32[1,32]{0,1:T(8,128)S(1)}, u32[]{:S(2)}, u32[]{:S(2)}) collective-permute-start(f32[1,32]{0,1:T(8,128)S(1)} %get-tuple-element.219), channel_id=1, source_target_pairs={{0,32},{32,64},{64,96},{96,128},{128,160},{160,192},{192,224},{1,3... | collective-permute-start | bytes 392 | tf_op jit(solution)/shard_map/ppermute | solution.py:22
  307.6 13.3 %collective-permute-start.42 = (f32[64,1]{0,1:T(1,128)S(1)}, f32[64,1]{0,1:T(1,128)S(1)}, u32[]{:S(2)}, u32[]{:S(2)}) collective-permute-start(f32[64,1]{0,1:T(1,128)S(1)} %get-tuple-element.217), channel_id=1, source_target_pairs={{0,1},{1,2},{2,3},{3,4},{4,5},{5,6},{6,7},{7,8},{8,9},{9,10},{10,1... | collective-permute-start | bytes 776 | tf_op jit(solution)/shard_map/ppermute | solution.py:22
  309.5 11.4 %collective-permute-start.43 = (f32[64,1]{0,1:T(1,128)S(1)}, f32[64,1]{0,1:T(1,128)S(1)}, u32[]{:S(2)}, u32[]{:S(2)}) collective-permute-start(f32[64,1]{0,1:T(1,128)S(1)} %get-tuple-element.218), channel_id=1, source_target_pairs={{1,0},{2,1},{3,2},{4,3},{5,4},{6,5},{7,6},{8,7},{9,8},{10,9},{11,1... | collective-permute-start | bytes 776 | tf_op jit(solution)/shard_map/ppermute | solution.py:23
  322.2 17.1 %collective-permute-start.46 = (f32[128,1]{1,0:T(8,128)S(1)}, f32[128,1]{1,0:T(8,128)S(1)}, u32[]{:S(2)}, u32[]{:S(2)}) collective-permute-start(f32[128,1]{1,0:T(8,128)S(1)} %get-tuple-element.205), channel_id=1, source_target_pairs={{0,1},{1,2},{2,3},{3,4},{4,5},{5,6},{6,7},{7,8},{8,9},{9,10},{10,1... | collective-permute-start | bytes 1544 | tf_op jit(solution)/shard_map/ppermute | solution.py:22
  324.1 15.2 %collective-permute-start.47 = (f32[128,1]{1,0:T(8,128)S(1)}, f32[128,1]{1,0:T(8,128)S(1)}, u32[]{:S(2)}, u32[]{:S(2)}) collective-permute-start(f32[128,1]{1,0:T(8,128)S(1)} %get-tuple-element.206), channel_id=1, source_target_pairs={{1,0},{2,1},{3,2},{4,3},{5,4},{6,5},{7,6},{8,7},{9,8},{10,9},{11,1... | collective-permute-start | bytes 1544 | tf_op jit(solution)/shard_map/ppermute | solution.py:23
  340.9 16.5 %collective-permute-start.50 = (f32[256,1]{1,0:T(8,128)S(1)}, f32[256,1]{1,0:T(8,128)S(1)}, u32[]{:S(2)}, u32[]{:S(2)}) collective-permute-start(f32[256,1]{1,0:T(8,128)S(1)} %get-tuple-element.193), channel_id=1, source_target_pairs={{0,1},{1,2},{2,3},{3,4},{4,5},{5,6},{6,7},{7,8},{8,9},{9,10},{10,1... | collective-permute-start | bytes 3080 | tf_op jit(solution)/shard_map/ppermute | solution.py:22
  343.1 14.4 %collective-permute-start.51 = (f32[256,1]{1,0:T(8,128)S(1)}, f32[256,1]{1,0:T(8,128)S(1)}, u32[]{:S(2)}, u32[]{:S(2)}) collective-permute-start(f32[256,1]{1,0:T(8,128)S(1)} %get-tuple-element.194), channel_id=1, source_target_pairs={{1,0},{2,1},{3,2},{4,3},{5,4},{6,5},{7,6},{8,7},{9,8},{10,9},{11,1... | collective-permute-start | bytes 3080 | tf_op jit(solution)/shard_map/ppermute | solution.py:23
  359.4 17.8 %collective-permute-start.54 = (f32[512,1]{0,1:T(1,128)S(1)}, f32[512,1]{0,1:T(1,128)S(1)}, u32[]{:S(2)}, u32[]{:S(2)}) collective-permute-start(f32[512,1]{0,1:T(1,128)S(1)} %get-tuple-element.175), channel_id=1, source_target_pairs={{0,1},{1,2},{2,3},{3,4},{4,5},{5,6},{6,7},{7,8},{8,9},{9,10},{10,1... | collective-permute-start | bytes 6152 | tf_op jit(solution)/shard_map/ppermute | solution.py:22
  361.3 15.9 %collective-permute-start.55 = (f32[512,1]{0,1:T(1,128)S(1)}, f32[512,1]{0,1:T(1,128)S(1)}, u32[]{:S(2)}, u32[]{:S(2)}) collective-permute-start(f32[512,1]{0,1:T(1,128)S(1)} %get-tuple-element.176), channel_id=1, source_target_pairs={{1,0},{2,1},{3,2},{4,3},{5,4},{6,5},{7,6},{8,7},{9,8},{10,9},{11,1... | collective-permute-start | bytes 6152 | tf_op jit(solution)/shard_map/ppermute | solution.py:23
  370.3 6.9 %collective-permute-start.53 = (f32[1,256]{0,1:T(8,128)S(1)}, f32[1,256]{0,1:T(8,128)S(1)}, u32[]{:S(2)}, u32[]{:S(2)}) collective-permute-start(f32[1,256]{0,1:T(8,128)S(1)} %get-tuple-element.178), channel_id=1, source_target_pairs={{32,0},{64,32},{96,64},{128,96},{160,128},{192,160},{224,192},{33,... | collective-permute-start | bytes 3080 | tf_op jit(solution)/shard_map/ppermute | solution.py:23
  379.0 17.8 %collective-permute-start.58 = (f32[512,1]{0,1:T(1,128)S(1)}, f32[512,1]{0,1:T(1,128)S(1)}, u32[]{:S(2)}, u32[]{:S(2)}) collective-permute-start(f32[512,1]{0,1:T(1,128)S(1)} %get-tuple-element.171), channel_id=1, source_target_pairs={{0,1},{1,2},{2,3},{3,4},{4,5},{5,6},{6,7},{7,8},{8,9},{9,10},{10,1... | collective-permute-start | bytes 6152 | tf_op jit(solution)/shard_map/ppermute | solution.py:22
  380.9 15.9 %collective-permute-start.59 = (f32[512,1]{0,1:T(1,128)S(1)}, f32[512,1]{0,1:T(1,128)S(1)}, u32[]{:S(2)}, u32[]{:S(2)}) collective-permute-start(f32[512,1]{0,1:T(1,128)S(1)} %get-tuple-element.172), channel_id=1, source_target_pairs={{1,0},{2,1},{3,2},{4,3},{5,4},{6,5},{7,6},{8,7},{9,8},{10,9},{11,1... | collective-permute-start | bytes 6152 | tf_op jit(solution)/shard_map/ppermute | solution.py:23
  (35 other events, 1367.7 us)
where the time goes:
time: 402 us; the launch traced here: 400 us
  starting transfers between devices  195 us (49%)
  local copies, waits for them, and re-layouts  112 us (28%)
  other arithmetic  54.6 us (14%)
  waiting for transfers between devices  35.6 us (9%)
    ppermute x28, starting transfers between devices, padded(): lax.ppermute(initial, axis, [(b, a) for a, b in up])  91.1 us
    ppermute x28, starting transfers between devices, padded(): lax.ppermute(last, axis, up)  90.9 us
    reshape x5, local copies, waits for them, and re-layouts, mean_blocks(): return field.reshape(height // 2, 2, width // 2, 2).sum(axis=(1, 3)) * 0.25  82.8 us
    reduce_sum x8, other arithmetic, mean_blocks(): return field.reshape(height // 2, 2, width // 2, 2).sum(axis=(1, 3)) * 0.25  38.2 us
    ppermute x28, waiting for transfers between devices, padded(): lax.ppermute(initial, axis, [(b, a) for a, b in up])  27.4 us
    mul x4, local copies, waits for them, and re-layouts, mean_blocks(): return field.reshape(height // 2, 2, width // 2, 2).sum(axis=(1, 3)) * 0.25  13.3 us
    add x17, other arithmetic, jacobi_step(): middle + relaxation * (source - apply_operator(field_pad, coeffs)) / coef...  9.42 us
  transfers between devices with their start and end apart: 60, of which 12 were waited for; matrix products, arithmetic and copies ran while one was open for 37% of the time, Pallas kernels for 0%

commit v1 on v0

v1 whole, which is shorter than its diff:
```python
import functools

import jax
import jax.numpy as jnp
from jax import lax
from jax.experimental import pallas as pl
from jax.experimental.pallas import tpu as pltpu
from jax.sharding import PartitionSpec as P

LEVELS = 4
SWEEPS = 12
DAMPING = 0.01
RELAX = 0.8
MESH = pl.DeviceIdType.MESH

LANES = 128
HALO = 24
BASE = 8
CHUNK = 40


def lane_of(shape):
    return lax.broadcasted_iota(jnp.int32, shape, len(shape) - 1)


def from_west(xs):
    rolled = [pltpu.roll(x, 1, 1) for x in xs]
    if len(xs) == 1:
        return rolled
    edge = lane_of(xs[0].shape) == 0
    return [jnp.where(edge, rolled[k - 1], rolled[k]) for k in range(len(xs))]


def from_east(xs):
    rolled = [pltpu.roll(x, LANES - 1, 1) for x in xs]
    if len(xs) == 1:
        return rolled
    edge = lane_of(xs[0].shape) == LANES - 1
    return [jnp.where(edge, rolled[(k + 1) % len(xs)], rolled[k]) for k in range(len(xs))]


def column(shape, axis, first, wrap, total):
    lane = lax.broadcasted_iota(jnp.int32, shape, axis) + first
    return jnp.where(lane < wrap, lane, lane - total)


def split_dot(x, matrix):
    high = x.astype(jnp.bfloat16)
    rest = x - high.astype(jnp.float32)
    mid = rest.astype(jnp.bfloat16)
    low = (rest - mid.astype(jnp.float32)).astype(jnp.bfloat16)
    dot = functools.partial(jnp.dot, preferred_element_type=jnp.float32)
    return dot(high, matrix) + dot(mid, matrix) + dot(low, matrix)


class Level:
    def __init__(self, rows, cols, ext):
        self.ext = ext
        self.n = rows + 2 * ext
        self.steps = -(-self.n // 8) * 8
        self.alloc = self.steps + 2 * BASE
        self.k = -(-(cols + 2 * ext) // LANES)
        self.total = self.k * LANES
        self.wrap = (self.total + cols) // 2

    def columns(self, shape, axis, first=0):
        return column(shape, axis, first, self.wrap, self.total)


def edges_and_diagonal(wref, k_count, at, n):
    w = [wref[k, pl.ds(at, n), :] for k in range(k_count)]
    south = [jnp.minimum(w[k], wref[k, pl.ds(at + 1, n), :]) for k in range(k_count)]
    north = [jnp.minimum(w[k], wref[k, pl.ds(at - 1, n), :]) for k in range(k_count)]
    beside = from_east(w)
    east = [jnp.minimum(w[k], beside[k]) for k in range(k_count)]
    west = from_west(east)
    diagonal = [DAMPING + (south[k] + north[k]) + (east[k] + west[k]) for k in range(k_count)]
    return north, south, east, west, diagonal


def residual(field, sref, east_ref, south_ref, k_count, at, n):
    v = [field[k, pl.ds(at, n), :] for k in range(k_count)]
    beside = from_east(v)
    flow = [east_ref[k, pl.ds(at, n), :] * (beside[k] - v[k]) for k in range(k_count)]
    back = from_west(flow)
    out = []
    for k in range(k_count):
        down = south_ref[k, pl.ds(at, n), :] * (field[k, pl.ds(at + 1, n), :] - v[k])
        up = south_ref[k, pl.ds(at - 1, n), :] * (field[k, pl.ds(at - 1, n), :] - v[k])
        inner = sref[k, pl.ds(at, n), :] - DAMPING * v[k]
        out.append(inner + (flow[k] - back[k]) + (down + up))
    return out, v


def over_rows(rows, chunk, body):
    if rows == chunk:
        body(BASE)
        return

    def step(i, carry):
        body(pl.multiple_of(BASE + i * chunk, 8))
        return carry

    lax.fori_loop(0, rows // chunk, step, 0)


def kernel(
    grid_rows,
    grid_cols,
    levels,
    rhs_hbm,
    pressure_hbm,
    wet_hbm,
    bathy_hbm,
    out_ref,
    res_ref,
    rhs_in,
    pressure_in,
    wet_in,
    bathy_in,
    fields,
    pack_east,
    pack_west,
    got_west,
    got_east,
    *scratch,
):
    scratch = list(scratch)
    take = lambda count: [scratch.pop(0) for _ in range(count)]
    w_refs = [fields.at[0]] + take(3)
    s_refs = [fields.at[1]] + take(3)
    v_refs = take(4)
    inv_refs = take(4)
    east_refs = take(4)
    south_refs = take(4)
    u_refs = take(4)
    own, wide = take(2)
    in_sem, send_sem, recv_sem, send2_sem, recv2_sem = take(5)
    g_ref = fields.at[2]
    rows, cols = rhs_in.shape
    fine = levels[0]

    gx, gy = lax.axis_index("gx"), lax.axis_index("gy")
    north = lax.rem(gx + grid_rows - 1, grid_rows)
    south = lax.rem(gx + 1, grid_rows)
    west = lax.rem(gy + grid_cols - 1, grid_cols)
    east = lax.rem(gy + 1, grid_cols)
    around = [
        (gx, east),
        (gx, west),
        (south, gy),
        (north, gy),
        (south, east),
        (north, east),
        (south, west),
        (north, west),
    ]
    barrier = pltpu.get_barrier_semaphore()
    for device in around:
        pl.semaphore_signal(barrier, inc=1, device_id=device, device_id_type=MESH)

    loads = [
        pltpu.make_async_copy(src, dst, in_sem.at[i])
        for i, (src, dst) in enumerate(
            ((wet_hbm, wet_in), (bathy_hbm, bathy_in), (rhs_hbm, rhs_in), (pressure_hbm, pressure_in))
        )
    ]
    for load in loads:
        load.start()

    has_north = (gx > 0).astype(jnp.float32)
    has_south = (gx < grid_rows - 1).astype(jnp.float32)
    has_west = (gy > 0).astype(jnp.float32)
    has_east = (gy < grid_cols - 1).astype(jnp.float32)

    def clear(ref, level):
        for k in range(level.k):
            ref[k, 0:BASE, :] = jnp.zeros((BASE, LANES), jnp.float32)
            tail = level.alloc - BASE - level.n
            ref[k, BASE + level.n : level.alloc, :] = jnp.zeros((tail, LANES), jnp.float32)

    clear(g_ref, fine)
    for i, level in enumerate(levels):
        for refs in (w_refs, s_refs, v_refs, south_refs, u_refs):
            clear(refs[i], level)

    for load in loads:
        load.wait()

    first = BASE + HALO

    prep = 64
    lane = lane_of((prep, LANES))

    def prepare(i, carry):
        at = pl.multiple_of(i * prep, 8)
        to = pl.multiple_of(first + i * prep, 8)
        made = []
        for k in range(2):
            part = slice(k * LANES, (k + 1) * LANES)
            wet = wet_in[pl.ds(at, prep), part].astype(jnp.float32)
            bathy = bathy_in[pl.ds(at, prep), part].astype(jnp.float32)
            w = wet * (1.0 + 0.5 * bathy)
            s = wet * rhs_in[pl.ds(at, prep), part]
            g = wet * pressure_in[pl.ds(at, prep), part]
            fields[0, k, pl.ds(to, prep), :] = w
            fields[1, k, pl.ds(to, prep), :] = s
            fields[2, k, pl.ds(to, prep), :] = g
            made.append((w, s, g))
        w, s, g = made[1]
        packed = jnp.where(lane >= LANES - HALO, w, pltpu.roll(s, LANES - HALO, 1))
        pack_east[pl.ds(at, prep), :] = jnp.where(
            lane >= LANES - 2 * HALO, packed, pltpu.roll(g, LANES - 2 * HALO, 1)
        )
        w, s, g = made[0]
        packed = jnp.where(lane < HALO, w, pltpu.roll(s, HALO, 1))
        pack_west[pl.ds(at, prep), :] = jnp.where(lane < 2 * HALO, packed, pltpu.roll(g, 2 * HALO, 1))
        return carry

    lax.fori_loop(0, rows // prep, prepare, 0)

    pl.semaphore_wait(barrier, len(around))

    top = slice(BASE, BASE + HALO)
    middle = slice(first, first + rows)
    bottom = slice(first + rows, first + rows + HALO)
    head, tail = slice(0, HALO), slice(rows - HALO, rows)
    mine_head = slice(first, first + HALO)
    mine_tail = slice(first + rows - HALO, first + rows)
    strips = [
        (pack_east, got_west.at[middle]),
        (pack_west, got_east.at[middle]),
        (fields.at[:, 0:2, mine_tail], fields.at[:, 0:2, top]),
        (fields.at[:, 0:2, mine_head], fields.at[:, 0:2, bottom]),
        (pack_east.at[tail], got_west.at[top]),
        (pack_east.at[head], got_west.at[bottom]),
        (pack_west.at[tail], got_east.at[top]),
        (pack_west.at[head], got_east.at[bottom]),
    ]
    copies = [
        pltpu.make_async_remote_copy(
            src_ref=src,
            dst_ref=dst,
            send_sem=send_sem.at[i],
            recv_sem=recv_sem.at[i],
            device_id=around[i],
            device_id_type=MESH,
        )
        for i, (src, dst) in enumerate(strips)
    ]
    for copy in copies:
        copy.start()
    for copy in copies:
        copy.wait()

    part = 56
    lane_part = lane_of((part, LANES))

    def unpack(i, carry):
        at = pl.multiple_of(BASE + i * part, 8)
        a = got_west[pl.ds(at, part), :]
        b = got_east[pl.ds(at, part), :]
        left = lane_part >= LANES // 2
        w = jnp.where(lane_part < HALO, b * has_east, 0.0)
        fields[0, 2, pl.ds(at, part), :] = jnp.where(lane_part >= LANES - HALO, a * has_west, w)
        fields[1, 2, pl.ds(at, part), :] = jnp.where(
            left, pltpu.roll(a, HALO, 1), pltpu.roll(b, LANES - HALO, 1)
        )
        fields[2, 2, pl.ds(at, part), :] = jnp.where(
            left, pltpu.roll(a, 2 * HALO, 1), pltpu.roll(b, LANES - 2 * HALO, 1)
        )
        return carry

    lax.fori_loop(0, fine.n // part, unpack, 0)
    for k in range(3):
        fields[0, k, top, :] = fields[0, k, top, :] * has_north
        fields[0, k, bottom, :] = fields[0, k, bottom, :] * has_south

    def restrict_map(level, coarse_cols, k_in, first_in, scale):
        shape = (k_in * LANES, LANES)
        hit = (level.columns(shape, 0, first_in * LANES) >> 1) == coarse_cols(shape)
        return jnp.where(hit, scale, 0.0).astype(jnp.bfloat16)

    def restrict_plan(l):
        if l == 0:
            return [(0, 2, 0), (2, 1, 1)]
        return [(0, levels[l].k, 0)]

    def restrict(ref, l, start, count, scale, coarse_cols):
        out = []
        for k0, k_in, k_out in restrict_plan(l):
            sums = [
                ref[k, pl.ds(start, count, stride=2), :] + ref[k, pl.ds(start + 1, count, stride=2), :]
                for k in range(k0, k0 + k_in)
            ]
            x = sums[0] if k_in == 1 else jnp.concatenate(sums, axis=1)
            matrix = restrict_map(levels[l], functools.partial(coarse_cols, k_out), k_in, k0, scale)
            out.append(split_dot(x, matrix))
        return out

    def coarse_columns(l):
        if l == LEVELS - 1:
            return lambda k, shape: lax.broadcasted_iota(jnp.int32, shape, 1) & (cols // 2**LEVELS - 1)
        return lambda k, shape: levels[l + 1].columns(shape, 1, k * LANES)

    tile_rows = rows // 2**LEVELS

    def send_tile(f):
        half = tile_rows // 2
        all_rows, up_rows, down_rows = slice(0, tile_rows), slice(0, half), slice(half, tile_rows)
        mid, above, below = slice(half, half + tile_rows), slice(0, half), slice(half + tile_rows, 2 * tile_rows)
        plan = [
            (all_rows, 0, mid),
            (all_rows, 2, mid),
            (down_rows, 1, above),
            (up_rows, 1, below),
            (down_rows, 0, above),
            (up_rows, 0, below),
            (down_rows, 2, above),
            (up_rows, 2, below),
        ]
        out = [
            pltpu.make_async_remote_copy(
                src_ref=own.at[f, src],
                dst_ref=wide.at[f, which, dst],
                send_sem=send2_sem.at[f, i],
                recv_sem=recv2_sem.at[f, i],
                device_id=around[i],
                device_id_type=MESH,
            )
            for i, (src, which, dst) in enumerate(plan)
        ]
        for copy in out:
            copy.start()
        return out

    for l in range(LEVELS - 1):
        level = levels[l]
        made = restrict(w_refs[l], l, BASE, level.n // 2, 0.125, coarse_columns(l))
        for k in range(levels[l + 1].k):
            w_refs[l + 1][k, pl.ds(BASE, level.n // 2), :] = made[k]
    last = levels[LEVELS - 1]
    tile = restrict(
        w_refs[LEVELS - 1], LEVELS - 1, BASE + last.ext, tile_rows, 0.125, coarse_columns(LEVELS - 1)
    )[0]
    own[0, :, :] = tile
    wide[0, 1, pl.ds(tile_rows // 2, tile_rows), :] = tile
    weight_copies = send_tile(0)

    def chunk_of(level):
        return CHUNK if level.steps % CHUNK == 0 and level.k > 1 else level.steps

    for l in range(LEVELS):
        level = levels[l]
        k_count = level.k
        n = chunk_of(level)

        def smooth(at):
            up, down, right, left, diagonal = edges_and_diagonal(w_refs[l], k_count, at, n)
            for k in range(k_count):
                inverse = RELAX / diagonal[k]
                inv_refs[l][k, pl.ds(at, n), :] = inverse
                east_refs[l][k, pl.ds(at, n), :] = right[k]
                south_refs[l][k, pl.ds(at, n), :] = down[k]
                if l > 0:
                    v_refs[l][k, pl.ds(at, n), :] = inverse * s_refs[l][k, pl.ds(at, n), :]
            if l == 0:
                g = [g_ref[k, pl.ds(at, n), :] for k in range(k_count)]
                beside = from_east(g)
                flow = [right[k] * (beside[k] - g[k]) for k in range(k_count)]
                back = from_west(flow)
                for k in range(k_count):
                    below = down[k] * (g_ref[k, pl.ds(at + 1, n), :] - g[k])
                    above = up[k] * (g_ref[k, pl.ds(at - 1, n), :] - g[k])
                    inner = s_refs[0][k, pl.ds(at, n), :] - DAMPING * g[k]
                    total = inner + (flow[k] - back[k]) + (below + above)
                    v_refs[0][k, pl.ds(at, n), :] = g[k] + (RELAX / diagonal[k]) * total

        over_rows(level.steps, n, smooth)

        def to_residual(at):
            out, _ = residual(v_refs[l], s_refs[l], east_refs[l], south_refs[l], k_count, at, n)
            for k in range(k_count):
                u_refs[l][k, pl.ds(at, n), :] = out[k]

        over_rows(level.steps, n, to_residual)
        if l < LEVELS - 1:
            made = restrict(u_refs[l], l, BASE, level.n // 2, 0.25, coarse_columns(l))
            for k in range(levels[l + 1].k):
                s_refs[l + 1][k, pl.ds(BASE, level.n // 2), :] = made[k]
        else:
            tile = restrict(u_refs[l], l, BASE + last.ext, tile_rows, 0.25, coarse_columns(l))[0]
            own[1, :, :] = tile
            wide[1, 1, pl.ds(tile_rows // 2, tile_rows), :] = tile
    source_copies = send_tile(1)

    for copy in weight_copies:
        copy.wait()
    tile_cols = cols // 2**LEVELS
    wide_rows = 2 * tile_rows
    lane_wide = lane_of((wide_rows, LANES))
    row_wide = lax.broadcasted_iota(jnp.int32, (wide_rows, LANES), 0)

    def merged(f, a, b):
        x = jnp.where(lane_wide < 2 * tile_cols, wide[f, 2] * b, 0.0)
        x = jnp.where(lane_wide < tile_cols, wide[f, 1], x)
        return jnp.where(lane_wide >= LANES - tile_cols, wide[f, 0] * a, x)

    w = merged(0, has_west, has_east)
    w = jnp.where(row_wide < tile_rows // 2, w * has_north, w)
    w = jnp.where(row_wide >= tile_rows + tile_rows // 2, w * has_south, w)

    def roll_rows(x, shift):
        return pltpu.roll(x, shift % wide_rows, 0)

    c_south = jnp.minimum(w, roll_rows(w, -1))
    c_north = roll_rows(c_south, 1)
    c_east = jnp.minimum(w, pltpu.roll(w, LANES - 1, 1))
    c_west = pltpu.roll(c_east, 1, 1)
    inverse = RELAX / (DAMPING + (c_south + c_north) + (c_east + c_west))
    for copy in source_copies:
        copy.wait()
    source = merged(1, 1.0, 1.0) * inverse
    a_south, a_north, a_east, a_west = (c * inverse for c in (c_south, c_north, c_east, c_west))

    def sweep(current):
        rows_part = a_south * roll_rows(current, -1) + a_north * roll_rows(current, 1)
        lanes_part = a_east * pltpu.roll(current, LANES - 1, 1) + a_west * pltpu.roll(current, 1, 1)
        return ((1.0 - RELAX) * current + source) + (rows_part + lanes_part)

    current = source
    for _ in range(SWEEPS - 1):
        current = sweep(current)

    for l in range(LEVELS - 1, -1, -1):
        level = levels[l]
        k_count = level.k
        n = chunk_of(level)
        if l == LEVELS - 1:
            lead = (level.ext + 1) // 2
            count = (level.n + 2) // 2
            wide[0, 0, :, :] = current
            coarse = [wide[0, 0, pl.ds(tile_rows // 2 - lead, count), :]]
            start = BASE + level.ext - 2 * lead
            coarse_col = lambda shape: column(shape, 0, 0, LANES // 2, LANES)
            plan = [(0, 1, 0)]
        else:
            count = level.n // 2
            coarse = [v_refs[l + 1][k, pl.ds(BASE, count), :] for k in range(levels[l + 1].k)]
            start = BASE
            plan = [(0, 2, 0), (2, 1, 1)] if l == 0 else [(0, k_count, None)]
        for k0, k_out, k_from in plan:
            if l < LEVELS - 1:
                source_level = levels[l + 1]
                if k_from is None:
                    x = coarse[0] if len(coarse) == 1 else jnp.concatenate(coarse, axis=1)
                    first_lane = 0
                else:
                    x, first_lane = coarse[k_from], k_from * LANES
                coarse_col = lambda shape: source_level.columns(shape, 0, first_lane)
            else:
                x = coarse[0]
            shape = (x.shape[1], k_out * LANES)
            hit = (level.columns(shape, 1, k0 * LANES) >> 1) == coarse_col(shape)
            spread = split_dot(x, jnp.where(hit, 1.0, 0.0).astype(jnp.bfloat16))
            for k in range(k_out):
                add = spread[:, k * LANES : (k + 1) * LANES]
                for side in range(2):
                    at = pl.ds(start + side, count, stride=2)
                    u_refs[l][k0 + k, at, :] = v_refs[l][k0 + k, at, :] + add

        def correct(at):
            out, v = residual(u_refs[l], s_refs[l], east_refs[l], south_refs[l], k_count, at, n)
            for k in range(k_count):
                v_refs[l][k, pl.ds(at, n), :] = v[k] + inv_refs[l][k, pl.ds(at, n), :] * out[k]

        over_rows(level.steps, n, correct)

    def finish(i, carry):
        at = pl.multiple_of(first + i * 32, 8)
        to = pl.multiple_of(i * 32, 8)
        out, v = residual(v_refs[0], s_refs[0], east_refs[0], south_refs[0], 3, at, 32)
        for k in range(2):
            out_ref[pl.ds(to, 32), k * LANES : (k + 1) * LANES] = v[k]
            res_ref[pl.ds(to, 32), k * LANES : (k + 1) * LANES] = out[k]
        return carry

    lax.fori_loop(0, rows // 32, finish, 0)


def local(grid_rows, grid_cols, rhs, pressure, wet_mask, bathy_class):
    rows, cols = rhs.shape
    levels = [Level(rows >> l, cols >> l, HALO >> l) for l in range(LEVELS)]
    f32 = jnp.float32
    vmem = lambda *shape: pltpu.VMEM(shape, f32)
    per_level = [vmem(level.k, level.alloc, LANES) for level in levels]
    tile_rows = rows // 2**LEVELS
    scratch = [
        vmem(rows, cols),
        vmem(rows, cols),
        pltpu.VMEM((rows, cols), jnp.int32),
        pltpu.VMEM((rows, cols), jnp.int32),
        vmem(3, levels[0].k, levels[0].alloc, LANES),
        vmem(rows, LANES),
        vmem(rows, LANES),
        vmem(levels[0].alloc, LANES),
        vmem(levels[0].alloc, LANES),
        *per_level[1:],
        *per_level[1:],
        *per_level,
        *per_level,
        *per_level,
        *per_level,
        *per_level,
        vmem(2, tile_rows, LANES),
        vmem(2, 3, 2 * tile_rows, LANES),
        pltpu.SemaphoreType.DMA((4,)),
        pltpu.SemaphoreType.DMA((8,)),
        pltpu.SemaphoreType.DMA((8,)),
        pltpu.SemaphoreType.DMA((2, 8)),
        pltpu.SemaphoreType.DMA((2, 8)),
    ]
    return pl.pallas_call(
        functools.partial(kernel, grid_rows, grid_cols, levels),
        out_shape=[jax.ShapeDtypeStruct((rows, cols), f32)] * 2,
        in_specs=[pl.BlockSpec(memory_space=pl.ANY)] * 4,
        out_specs=[pl.BlockSpec(memory_space=pltpu.VMEM)] * 2,
        scratch_shapes=scratch,
        compiler_params=pltpu.CompilerParams(
            collective_id=0, has_side_effects=True, vmem_limit_bytes=48 * 1024 * 1024
        ),
    )(rhs, pressure, wet_mask, bathy_class)


def solution(mesh):
    placed = P("gx", "gy")
    body = functools.partial(local, mesh.shape["gx"], mesh.shape["gy"])
    return jax.shard_map(
        lambda *args: tuple(body(*args)),
        mesh=mesh,
        in_specs=(placed,) * 4,
        out_specs=(placed,) * 2,
        check_vma=False,
    )
```

time: 402 us -> 46.1 us (0.11)
  the two profiles are of different devices: /device:TPU:8 before, /device:TPU:32 now
where the time goes in v1:
time: 46.1 us; the launch traced here: 45.8 us
  Pallas kernels  39.4 us (85%)
  local copies, waits for them, and re-layouts  5.75 us (12%)
  between operations  0.65 us (1%)
    pallas_call x1, Pallas kernels, local(): pl.pallas_call(functools.partial(kernel, grid_rows, grid_cols, levels), o...  39.4 us
    unnamed x10, local copies, waits for them, and re-layouts  5.75 us

profile of v1, /device:TPU:32, one launch (start us, length us, event | category | flops | bytes accessed | tf_op | source)
XLA Modules:
  0.0 45.8 jit_solution(5472918823278334940)
XLA Ops:
  0.6 0.0 copy-start
  0.6 1.0 %copy-done = f32[512,256]{1,0:T(8,128)S(1)} copy-done((f32[512,256]{1,0:T(8,128)S(1)}, f32[512,256]{1,0:T(8,128)}, u32[]{:S(2)}) %copy-start) | copy-done | bytes 524312
  1.7 0.0 copy-start.1
  1.7 1.0 %copy-done.1 = f32[512,256]{1,0:T(8,128)S(1)} copy-done((f32[512,256]{1,0:T(8,128)S(1)}, f32[512,256]{1,0:T(8,128)}, u32[]{:S(2)}) %copy-start.1) | copy-done | bytes 524312
  2.7 0.0 copy-start.2
  2.7 1.0 %copy-done.2 = s32[512,256]{1,0:T(8,128)S(1)} copy-done((s32[512,256]{1,0:T(8,128)S(1)}, s32[512,256]{1,0:T(8,128)}, u32[]{:S(2)}) %copy-start.2) | copy-done | bytes 524312
  3.8 0.0 copy-start.3
  3.8 1.0 %copy-done.3 = s32[512,256]{1,0:T(8,128)S(1)} copy-done((s32[512,256]{1,0:T(8,128)S(1)}, s32[512,256]{1,0:T(8,128)}, u32[]{:S(2)}) %copy-start.3) | copy-done | bytes 524312
  4.8 39.4 %shard_map.59 = (f32[512,256]{1,0:T(8,128)S(1)}, f32[512,256]{1,0:T(8,128)S(1)}) custom-call(f32[512,256]{1,0:T(8,128)S(1)} %copy-done, f32[512,256]{1,0:T(8,128)S(1)} %copy-done.1, s32[512,256]{1,0:T(8,128)S(1)} %copy-done.2, s32[512,256]{1,0:T(8,128)S(1)} %copy-done.3), custom_call_target="tpu_custom_call" | custom-call | tf_op jit(solution)/shard_map/pallas_call | solution.py:523
  44.3 0.8 %copy.8 = f32[512,256]{1,0:T(8,128)} copy(f32[512,256]{1,0:T(8,128)S(1)} %get-tuple-element.4) | data formatting | bytes 1048576
  45.1 0.8 %copy.9 = f32[512,256]{1,0:T(8,128)} copy(f32[512,256]{1,0:T(8,128)S(1)} %get-tuple-element.5) | data formatting | bytes 1048576
Async XLA Ops:
  0.6 1.0 %copy-start = (f32[512,256]{1,0:T(8,128)S(1)}, f32[512,256]{1,0:T(8,128)}, u32[]{:S(2)}) copy-start(f32[512,256]{1,0:T(8,128)} %rhs_hbm.1) | copy-start | bytes 1572868
  1.7 1.0 %copy-start.1 = (f32[512,256]{1,0:T(8,128)S(1)}, f32[512,256]{1,0:T(8,128)}, u32[]{:S(2)}) copy-start(f32[512,256]{1,0:T(8,128)} %pressure_hbm.1) | copy-start | bytes 1572868
  2.7 1.0 %copy-start.2 = (s32[512,256]{1,0:T(8,128)S(1)}, s32[512,256]{1,0:T(8,128)}, u32[]{:S(2)}) copy-start(s32[512,256]{1,0:T(8,128)} %wet_hbm.1) | copy-start | bytes 1572868
  3.8 1.0 %copy-start.3 = (s32[512,256]{1,0:T(8,128)S(1)}, s32[512,256]{1,0:T(8,128)}, u32[]{:S(2)}) copy-start(s32[512,256]{1,0:T(8,128)} %bathy_hbm.1) | copy-start | bytes 1572868

commit v2 on v1

--- a/solution.py
+++ b/solution.py
@@ -16,7 +16,6 @@
 LANES = 128
 HALO = 24
 BASE = 8
-CHUNK = 40
 
 
 def lane_of(shape):
@@ -189,12 +188,12 @@
 
     first = BASE + HALO
 
-    prep = 64
+    prep = rows
     lane = lane_of((prep, LANES))
 
     def prepare(i, carry):
-        at = pl.multiple_of(i * prep, 8)
-        to = pl.multiple_of(first + i * prep, 8)
+        at = i * prep
+        to = first + i * prep
         made = []
         for k in range(2):
             part = slice(k * LANES, (k + 1) * LANES)
@@ -217,7 +216,7 @@
         pack_west[pl.ds(at, prep), :] = jnp.where(lane < 2 * HALO, packed, pltpu.roll(g, 2 * HALO, 1))
         return carry
 
-    lax.fori_loop(0, rows // prep, prepare, 0)
+    prepare(0, 0)
 
     pl.semaphore_wait(barrier, len(around))
 
@@ -253,11 +252,11 @@
     for copy in copies:
         copy.wait()
 
-    part = 56
+    part = fine.n
     lane_part = lane_of((part, LANES))
 
     def unpack(i, carry):
-        at = pl.multiple_of(BASE + i * part, 8)
+        at = BASE + i * part
         a = got_west[pl.ds(at, part), :]
         b = got_east[pl.ds(at, part), :]
         left = lane_part >= LANES // 2
@@ -271,7 +270,7 @@
         )
         return carry
 
-    lax.fori_loop(0, fine.n // part, unpack, 0)
+    unpack(0, 0)
     for k in range(3):
         fields[0, k, top, :] = fields[0, k, top, :] * has_north
         fields[0, k, bottom, :] = fields[0, k, bottom, :] * has_south
@@ -348,7 +347,7 @@
     weight_copies = send_tile(0)
 
     def chunk_of(level):
-        return CHUNK if level.steps % CHUNK == 0 and level.k > 1 else level.steps
+        return level.steps
 
     for l in range(LEVELS):
         level = levels[l]
@@ -477,15 +476,15 @@
         over_rows(level.steps, n, correct)
 
     def finish(i, carry):
-        at = pl.multiple_of(first + i * 32, 8)
-        to = pl.multiple_of(i * 32, 8)
-        out, v = residual(v_refs[0], s_refs[0], east_refs[0], south_refs[0], 3, at, 32)
+        at = first + i * rows
+        to = i * rows
+        out, v = residual(v_refs[0], s_refs[0], east_refs[0], south_refs[0], 3, at, rows)
         for k in range(2):
-            out_ref[pl.ds(to, 32), k * LANES : (k + 1) * LANES] = v[k]
-            res_ref[pl.ds(to, 32), k * LANES : (k + 1) * LANES] = out[k]
+            out_ref[pl.ds(to, rows), k * LANES : (k + 1) * LANES] = v[k]
+            res_ref[pl.ds(to, rows), k * LANES : (k + 1) * LANES] = out[k]
         return carry
 
-    lax.fori_loop(0, rows // 32, finish, 0)
+    finish(0, 0)
 
 
 def local(grid_rows, grid_cols, rhs, pressure, wet_mask, bathy_class):
@@ -527,7 +526,7 @@
         out_specs=[pl.BlockSpec(memory_space=pltpu.VMEM)] * 2,
         scratch_shapes=scratch,
         compiler_params=pltpu.CompilerParams(
-            collective_id=0, has_side_effects=True, vmem_limit_bytes=48 * 1024 * 1024
+            collective_id=0, has_side_effects=True, vmem_limit_bytes=62 * 1024 * 1024
         ),
     )(rhs, pressure, wet_mask, bathy_class)
 

time: 46.1 us -> 32.7 us (0.71)
  Pallas kernels: 39.4 us -> 29.2 us
  local copies, waits for them, and re-layouts: 5.75 us -> 2.72 us
    pallas_call x1, Pallas kernels: 39.4 us -> 29.2 us  [local(): pl.pallas_call(functools.partial(kernel, grid_rows, grid_cols, levels), o...]
    unnamed x10 -> x4, local copies, waits for them, and re-layouts: 5.75 us -> 2.72 us
where the time goes in v2:
time: 32.7 us; the launch traced here: 32.6 us
  Pallas kernels  29.2 us (89%)
  local copies, waits for them, and re-layouts  2.72 us (8%)
  between operations  0.65 us (2%)
    pallas_call x1, Pallas kernels, local(): pl.pallas_call(functools.partial(kernel, grid_rows, grid_cols, levels), o...  29.2 us
    unnamed x4, local copies, waits for them, and re-layouts  2.72 us

profile of v2, /device:TPU:32, one launch (start us, length us, event | category | flops | bytes accessed | tf_op | source)
XLA Modules:
  0.0 32.6 jit_solution(17945938795772948562)
XLA Ops:
  0.6 29.2 %shard_map.59 = (f32[512,256]{1,0:T(8,128)}, f32[512,256]{1,0:T(8,128)}) custom-call(f32[512,256]{1,0:T(8,128)} %rhs_hbm.1, f32[512,256]{1,0:T(8,128)} %pressure_hbm.1, s32[512,256]{1,0:T(8,128)} %wet_hbm.1, s32[512,256]{1,0:T(8,128)} %bathy_hbm.1), custom_call_target="tpu_custom_call" | custom-call | tf_op jit(solution)/shard_map/pallas_call | solution.py:522
  29.9 0.0 copy-start
  29.9 1.9 %copy.8 = f32[512,256]{1,0:T(8,128)} copy(f32[512,256]{1,0:T(8,128)} %get-tuple-element.4) | data formatting | bytes 1048576
  31.8 0.0 copy-done
  31.8 0.8 %copy.9 = f32[512,256]{1,0:T(8,128)} copy(f32[512,256]{1,0:T(8,128)S(1)} %copy-done) | data formatting | bytes 1048576
Async XLA Ops:
  29.9 1.9 %copy-start = (f32[512,256]{1,0:T(8,128)S(1)}, f32[512,256]{1,0:T(8,128)}, u32[]{:S(2)}) copy-start(f32[512,256]{1,0:T(8,128)} %get-tuple-element.5) | copy-start | bytes 1572868

commit v3 on v2

--- a/solution.py
+++ b/solution.py
@@ -15,6 +15,7 @@
 
 LANES = 128
 HALO = 24
+PIECES = 2
 BASE = 8
 
 
@@ -111,13 +112,14 @@
     pressure_hbm,
     wet_hbm,
     bathy_hbm,
-    out_ref,
-    res_ref,
+    field_out,
+    fields,
+    east_out,
+    south_out,
     rhs_in,
     pressure_in,
     wet_in,
     bathy_in,
-    fields,
     pack_east,
     pack_west,
     got_west,
@@ -128,10 +130,10 @@
     take = lambda count: [scratch.pop(0) for _ in range(count)]
     w_refs = [fields.at[0]] + take(3)
     s_refs = [fields.at[1]] + take(3)
-    v_refs = take(4)
+    v_refs = [field_out] + take(3)
     inv_refs = take(4)
-    east_refs = take(4)
-    south_refs = take(4)
+    east_refs = [east_out] + take(3)
+    south_refs = [south_out] + take(3)
     u_refs = take(4)
     own, wide = take(2)
     in_sem, send_sem, recv_sem, send2_sem, recv2_sem = take(5)
@@ -154,9 +156,36 @@
         (south, west),
         (north, west),
     ]
+    at_north, at_south = gx == 0, gx == grid_rows - 1
+    at_west, at_east = gy == 0, gy == grid_cols - 1
+    inside = lambda *edges: functools.reduce(jnp.logical_and, [jnp.logical_not(edge) for edge in edges])
+    exists = [
+        inside(at_east),
+        inside(at_west),
+        inside(at_south),
+        inside(at_north),
+        inside(at_south, at_east),
+        inside(at_north, at_east),
+        inside(at_south, at_west),
+        inside(at_north, at_west),
+    ]
+    opposite = [1, 0, 3, 2, 7, 6, 5, 4]
     barrier = pltpu.get_barrier_semaphore()
-    for device in around:
-        pl.semaphore_signal(barrier, inc=1, device_id=device, device_id_type=MESH)
+    for i, device in enumerate(around):
+
+        @pl.when(exists[i])
+        def _():
+            pl.semaphore_signal(barrier, inc=1, device_id=device, device_id_type=MESH)
+
+    def start_all(copies):
+        for i, copy in enumerate(copies):
+            pl.when(exists[i])(copy.start)
+
+    def wait_all(copies):
+        for i, copy in enumerate(copies):
+            pl.when(exists[opposite[i]])(copy.wait_recv)
+        for i, copy in enumerate(copies):
+            pl.when(exists[i])(copy.wait_send)
 
     loads = [
         pltpu.make_async_copy(src, dst, in_sem.at[i])
@@ -167,11 +196,6 @@
     for load in loads:
         load.start()
 
-    has_north = (gx > 0).astype(jnp.float32)
-    has_south = (gx < grid_rows - 1).astype(jnp.float32)
-    has_west = (gy > 0).astype(jnp.float32)
-    has_east = (gy < grid_cols - 1).astype(jnp.float32)
-
     def clear(ref, level):
         for k in range(level.k):
             ref[k, 0:BASE, :] = jnp.zeros((BASE, LANES), jnp.float32)
@@ -182,6 +206,33 @@
     for i, level in enumerate(levels):
         for refs in (w_refs, s_refs, v_refs, south_refs, u_refs):
             clear(refs[i], level)
+
+    top = slice(BASE, BASE + HALO)
+    middle = slice(BASE + HALO, BASE + HALO + rows)
+    bottom = slice(BASE + HALO + rows, BASE + 2 * HALO + rows)
+    half = rows // 2 ** (LEVELS + 1)
+
+    def blank(ref, *index):
+        ref[index] = jnp.zeros(ref.at[index].shape, jnp.float32)
+
+    @pl.when(at_west)
+    def _():
+        blank(got_west, slice(None), slice(None))
+        blank(wide, slice(None), 0)
+
+    @pl.when(at_east)
+    def _():
+        blank(got_east, slice(None), slice(None))
+        blank(wide, slice(None), 2)
+
+    for edge, strip, wide_strip in ((at_north, top, slice(0, half)), (at_south, bottom, slice(3 * half, 4 * half))):
+
+        @pl.when(edge)
+        def _():
+            blank(got_west, strip, slice(None))
+            blank(got_east, strip, slice(None))
+            blank(fields, slice(None), slice(0, 2), strip)
+            blank(wide, slice(None), slice(None), wide_strip)
 
     for load in loads:
         load.wait()
@@ -218,11 +269,9 @@
 
     prepare(0, 0)
 
-    pl.semaphore_wait(barrier, len(around))
-
-    top = slice(BASE, BASE + HALO)
-    middle = slice(first, first + rows)
-    bottom = slice(first + rows, first + rows + HALO)
+    count = lambda low, high: 3 - low.astype(jnp.int32) - high.astype(jnp.int32)
+    pl.semaphore_wait(barrier, count(at_north, at_south) * count(at_west, at_east) - 1)
+
     head, tail = slice(0, HALO), slice(rows - HALO, rows)
     mine_head = slice(first, first + HALO)
     mine_tail = slice(first + rows - HALO, first + rows)
@@ -247,10 +296,8 @@
         )
         for i, (src, dst) in enumerate(strips)
     ]
-    for copy in copies:
-        copy.start()
-    for copy in copies:
-        copy.wait()
+    start_all(copies)
+    wait_all(copies)
 
     part = fine.n
     lane_part = lane_of((part, LANES))
@@ -260,8 +307,8 @@
         a = got_west[pl.ds(at, part), :]
         b = got_east[pl.ds(at, part), :]
         left = lane_part >= LANES // 2
-        w = jnp.where(lane_part < HALO, b * has_east, 0.0)
-        fields[0, 2, pl.ds(at, part), :] = jnp.where(lane_part >= LANES - HALO, a * has_west, w)
+        w = jnp.where(lane_part < HALO, b, 0.0)
+        fields[0, 2, pl.ds(at, part), :] = jnp.where(lane_part >= LANES - HALO, a, w)
         fields[1, 2, pl.ds(at, part), :] = jnp.where(
             left, pltpu.roll(a, HALO, 1), pltpu.roll(b, LANES - HALO, 1)
         )
@@ -271,9 +318,6 @@
         return carry
 
     unpack(0, 0)
-    for k in range(3):
-        fields[0, k, top, :] = fields[0, k, top, :] * has_north
-        fields[0, k, bottom, :] = fields[0, k, bottom, :] * has_south
 
     def restrict_map(level, coarse_cols, k_in, first_in, scale):
         shape = (k_in * LANES, LANES)
@@ -305,7 +349,6 @@
     tile_rows = rows // 2**LEVELS
 
     def send_tile(f):
-        half = tile_rows // 2
         all_rows, up_rows, down_rows = slice(0, tile_rows), slice(0, half), slice(half, tile_rows)
         mid, above, below = slice(half, half + tile_rows), slice(0, half), slice(half + tile_rows, 2 * tile_rows)
         plan = [
@@ -329,8 +372,7 @@
             )
             for i, (src, which, dst) in enumerate(plan)
         ]
-        for copy in out:
-            copy.start()
+        start_all(out)
         return out
 
     for l in range(LEVELS - 1):
@@ -393,21 +435,17 @@
             wide[1, 1, pl.ds(tile_rows // 2, tile_rows), :] = tile
     source_copies = send_tile(1)
 
-    for copy in weight_copies:
-        copy.wait()
+    wait_all(weight_copies)
     tile_cols = cols // 2**LEVELS
     wide_rows = 2 * tile_rows
     lane_wide = lane_of((wide_rows, LANES))
-    row_wide = lax.broadcasted_iota(jnp.int32, (wide_rows, LANES), 0)
-
-    def merged(f, a, b):
-        x = jnp.where(lane_wide < 2 * tile_cols, wide[f, 2] * b, 0.0)
+
+    def merged(f):
+        x = jnp.where(lane_wide < 2 * tile_cols, wide[f, 2], 0.0)
         x = jnp.where(lane_wide < tile_cols, wide[f, 1], x)
-        return jnp.where(lane_wide >= LANES - tile_cols, wide[f, 0] * a, x)
-
-    w = merged(0, has_west, has_east)
-    w = jnp.where(row_wide < tile_rows // 2, w * has_north, w)
-    w = jnp.where(row_wide >= tile_rows + tile_rows // 2, w * has_south, w)
+        return jnp.where(lane_wide >= LANES - tile_cols, wide[f, 0], x)
+
+    w = merged(0)
 
     def roll_rows(x, shift):
         return pltpu.roll(x, shift % wide_rows, 0)
@@ -417,9 +455,8 @@
     c_east = jnp.minimum(w, pltpu.roll(w, LANES - 1, 1))
     c_west = pltpu.roll(c_east, 1, 1)
     inverse = RELAX / (DAMPING + (c_south + c_north) + (c_east + c_west))
-    for copy in source_copies:
-        copy.wait()
-    source = merged(1, 1.0, 1.0) * inverse
+    wait_all(source_copies)
+    source = merged(1) * inverse
     a_south, a_north, a_east, a_west = (c * inverse for c in (c_south, c_north, c_east, c_west))
 
     def sweep(current):
@@ -475,16 +512,27 @@
 
         over_rows(level.steps, n, correct)
 
-    def finish(i, carry):
-        at = first + i * rows
-        to = i * rows
-        out, v = residual(v_refs[0], s_refs[0], east_refs[0], south_refs[0], 3, at, rows)
+
+def finish(field, fields, east_ref, south_ref, out_hbm, res_hbm, res, sem):
+    first = BASE + HALO
+    rows = out_hbm.shape[0]
+    copies = []
+
+    def send(src, hbm, at, n, k):
+        copies.append(pltpu.make_async_copy(src, hbm.at[at : at + n, k * LANES : (k + 1) * LANES], sem.at[len(copies)]))
+        copies[-1].start()
+
+    for k in range(2):
+        send(field.at[k, first : first + rows], out_hbm, 0, rows, k)
+    n = rows // PIECES
+    for at in range(0, rows, n):
+        out, _ = residual(field, fields.at[1], east_ref, south_ref, 3, first + at, n)
         for k in range(2):
-            out_ref[pl.ds(to, rows), k * LANES : (k + 1) * LANES] = v[k]
-            res_ref[pl.ds(to, rows), k * LANES : (k + 1) * LANES] = out[k]
-        return carry
-
-    finish(0, 0)
+            res[k, at : at + n, :] = out[k]
+        for k in range(2):
+            send(res.at[k, at : at + n], res_hbm, at, n, k)
+    for copy in copies:
+        copy.wait()
 
 
 def local(grid_rows, grid_cols, rhs, pressure, wet_mask, bathy_class):
@@ -499,17 +547,16 @@
         vmem(rows, cols),
         pltpu.VMEM((rows, cols), jnp.int32),
         pltpu.VMEM((rows, cols), jnp.int32),
-        vmem(3, levels[0].k, levels[0].alloc, LANES),
         vmem(rows, LANES),
         vmem(rows, LANES),
         vmem(levels[0].alloc, LANES),
         vmem(levels[0].alloc, LANES),
         *per_level[1:],
         *per_level[1:],
+        *per_level[1:],
         *per_level,
-        *per_level,
-        *per_level,
-        *per_level,
+        *per_level[1:],
+        *per_level[1:],
         *per_level,
         vmem(2, tile_rows, LANES),
         vmem(2, 3, 2 * tile_rows, LANES),
@@ -519,16 +566,26 @@
         pltpu.SemaphoreType.DMA((2, 8)),
         pltpu.SemaphoreType.DMA((2, 8)),
     ]
-    return pl.pallas_call(
+    block = (levels[0].k, levels[0].alloc, LANES)
+    struct = lambda *shape: jax.ShapeDtypeStruct(shape, f32)
+    held = pl.pallas_call(
         functools.partial(kernel, grid_rows, grid_cols, levels),
-        out_shape=[jax.ShapeDtypeStruct((rows, cols), f32)] * 2,
-        in_specs=[pl.BlockSpec(memory_space=pl.ANY)] * 4,
-        out_specs=[pl.BlockSpec(memory_space=pltpu.VMEM)] * 2,
+        out_shape=[struct(*block), struct(3, *block), struct(*block), struct(*block)],
+        in_specs=[pl.BlockSpec(memory_space=pltpu.HBM)] * 4,
+        out_specs=[pl.BlockSpec(memory_space=pltpu.VMEM)] * 4,
         scratch_shapes=scratch,
         compiler_params=pltpu.CompilerParams(
-            collective_id=0, has_side_effects=True, vmem_limit_bytes=62 * 1024 * 1024
+            collective_id=0, has_side_effects=True, vmem_limit_bytes=40 * 1024 * 1024
         ),
-    )(rhs, pressure, wet_mask, bathy_class)
+    )(*[pltpu.with_memory_space_constraint(x, pltpu.HBM) for x in (rhs, pressure, wet_mask, bathy_class)])
+    return pl.pallas_call(
+        finish,
+        out_shape=[struct(rows, cols)] * 2,
+        in_specs=[pl.BlockSpec(memory_space=pltpu.VMEM)] * 4,
+        out_specs=[pl.BlockSpec(memory_space=pltpu.HBM)] * 2,
+        scratch_shapes=[vmem(2, rows, LANES), pltpu.SemaphoreType.DMA((2 + 2 * PIECES,))],
+        compiler_params=pltpu.CompilerParams(vmem_limit_bytes=48 * 1024 * 1024),
+    )(*held)
 
 
 def solution(mesh):

time: 32.7 us -> 25.7 us (0.79)
  the two profiles are of different devices: /device:TPU:32 before, /device:TPU:88 now
where the time goes in v3:
time: 25.7 us; the launch traced here: 25.6 us
  Pallas kernels  24.9 us (97%)
  between operations  0.64 us (2%)
    pallas_call x1, Pallas kernels, local(): pl.pallas_call(functools.partial(kernel, grid_rows, grid_cols, levels), o...  23.6 us
    pallas_call x1, Pallas kernels, local(): pl.pallas_call(finish, out_shape=[struct(rows, cols)] * 2, in_specs=[pl.B...  1.34 us

profile of v3, /device:TPU:88, one launch (start us, length us, event | category | flops | bytes accessed | tf_op | source)
XLA Modules:
  0.0 25.6 jit_solution(14247014103758188130)
XLA Ops:
  0.6 23.6 %shard_map.59 = (f32[3,576,128]{2,1,0:T(8,128)S(1)}, f32[3,3,576,128]{3,2,1,0:T(8,128)S(1)}, f32[3,576,128]{2,1,0:T(8,128)S(1)}, f32[3,576,128]{2,1,0:T(8,128)S(1)}) custom-call(f32[512,256]{1,0:T(8,128)} %rhs_hbm.1, f32[512,256]{1,0:T(8,128)} %pressure_hbm.1, s32[512,256]{1,0:T(8,128)} %wet_hbm.1, s32[512,256]{1,0:T(8,128)} %bathy_hbm.1), custom_call_target="tpu_custom_call" | custom-call | tf_op jit(solution)/shard_map/pallas_call | solution.py:571
  24.2 1.3 %shard_map.60 = (f32[512,256]{1,0:T(8,128)}, f32[512,256]{1,0:T(8,128)}) custom-call(f32[3,576,128]{2,1,0:T(8,128)S(1)} %get-tuple-element.6.field, f32[3,3,576,128]{3,2,1,0:T(8,128)S(1)} %get-tuple-element.7.fields, f32[3,576,128]{2,1,0:T(8,128)S(1)} %get-tuple-element.8.east_ref, f32[3,576,128]{2,1,0:T(8,128)S(1)} %get-tuple-element.9.south_ref), custom_call_target="tpu_custom_call" | custom-call | tf_op jit(solution)/shard_map/pallas_call | solution.py:581
